TPU v7x, 256 devices: a whole 4x4x8 slice. The times are simulated.
256 devices in a mesh: fsdp: 8 (over y, core), expert: 32 (over z, x).
Axes of the slice: x: 4, y: 4, z: 8, core: 2. Of those that a mesh axis runs over, the one named last changes fastest.
Arguments:
- tokens: bfloat16 [4096, 4096], P(('fsdp', 'expert')), may hold values from -18 to 18
- learner_rows: bfloat16 [64, 3, 768, 4096], P(None, None, 'expert', 'fsdp'), may hold values from -0.25 to 0.25, as said below
- exponents: int32 [64, 3, 768, 128], P(None, None, 'expert', 'fsdp'), may hold values from -9 to -5
- expert_ids: int32 [4096, 8], P(('fsdp', 'expert')), may hold values from 0 to 63, all different within a row; in each aligned block of 16 rows (0 to 15, 16 to 31, ...) at most 4 rows name the same one
- route_probs: float32 [4096, 8], P(('fsdp', 'expert')), may hold values from 0.05 to 1
Outputs:
- rollout_elements: bfloat16 [64, 3, 768, 4096], P('expert', None, None, 'fsdp')
- mixed: bfloat16 [4096, 4096], P(('fsdp', 'expert'))
Inputs may be any that keep to these rules, and one draw needn't show every extreme that they name: `expert_ids`: each row names 8 different experts. Among the rows of one device no expert is named more than 4 times, a bound that some block reaches. `learner_rows`: each entry is at most 8 times its block's scale 2 ** exponent in magnitude.
All inputs are finite; a program needn't handle non-finite values.
Results may differ from a plain program's by a relative error of at most 0.02.
Values may be sent and summed in bfloat16 or wider, within the bound.
A program may use at most 128 MiB of HBM per device.

v0:
```python
import jax
import jax.numpy as jnp
from jax import lax
from jax.sharding import PartitionSpec as P

BLOCK = 32


def to_grid(ratio):
    clipped = jnp.clip(ratio.astype(jnp.float32), -6.0, 6.0)
    magnitude = jnp.abs(clipped)
    level = (
        0.5 * (magnitude > 0.25)
        + 0.5 * (magnitude >= 0.75)
        + 0.5 * (magnitude > 1.25)
        + 0.5 * (magnitude >= 1.75)
    )
    level = level + 1.0 * (magnitude > 2.5) + 1.0 * (magnitude >= 3.5) + 2.0 * (magnitude > 5.0)
    return (jnp.sign(clipped) * level.astype(jnp.float32)).astype(jnp.bfloat16)


def body(tokens, learner_rows, exponents, expert_ids, route_probs):
    experts, part_count, unit_rows, feat_cols = learner_rows.shape
    owners = lax.axis_size("expert")
    groups = lax.axis_size("fsdp")
    per_owner = experts // owners
    tok_rows, top_count = expert_ids.shape
    width = tokens.shape[1]
    capacity = 2 * tok_rows * top_count // experts
    scales = jnp.exp2(exponents.astype(jnp.float32)).astype(jnp.bfloat16)
    widened = jnp.repeat(scales, BLOCK, axis=3)
    elements = to_grid(learner_rows / widened)
    element_view = elements.reshape(owners, per_owner, part_count, unit_rows, feat_cols)
    scale_view = scales.reshape(owners, per_owner, part_count, unit_rows, feat_cols // BLOCK)
    flat_ids = expert_ids.reshape(-1)
    one_hot = (flat_ids[:, None] == jnp.arange(experts, dtype=jnp.int32)[None, :]).astype(jnp.int32)
    position = jnp.sum((jnp.cumsum(one_hot, axis=0) - one_hot) * one_hot, axis=1)
    slot_index = flat_ids * capacity + position
    picked = (
        slot_index[:, None] == jnp.arange(experts * capacity, dtype=jnp.int32)[None, :]
    ).astype(jnp.float32)
    picked = picked.reshape(tok_rows, top_count, experts * capacity)
    routing = jnp.sum(picked, axis=1).astype(jnp.bfloat16)
    route_share = route_probs / jnp.sum(route_probs, axis=1, keepdims=True)
    blend_table = jnp.sum(picked * route_share[:, :, None], axis=1)
    packed = lax.dot_general(
        routing, tokens, (((0,), (0,)), ((), ())), preferred_element_type=jnp.float32
    )
    packed_view = packed.astype(jnp.bfloat16).reshape(owners, per_owner, 1, capacity, width)
    element_got, scale_got = (
        lax.all_to_all(element_view, "expert", split_axis=0, concat_axis=3, tiled=True),
        lax.all_to_all(scale_view, "expert", split_axis=0, concat_axis=3, tiled=True),
    )
    slot_got = lax.all_to_all(
        lax.all_to_all(packed_view, "fsdp", split_axis=4, concat_axis=3, tiled=True),
        "expert",
        split_axis=0,
        concat_axis=3,
        tiled=True,
    )
    weights = element_got[0] * jnp.repeat(scale_got[0], BLOCK, axis=3)
    slot_rows = slot_got[0, :, 0]
    paired = weights[:, 0:2]
    down_rows = weights[:, 2]
    partial_value = jnp.einsum(
        "ksd,kghd->ksgh", slot_rows, paired, preferred_element_type=jnp.float32
    )
    summed = lax.psum_scatter(
        partial_value.astype(jnp.bfloat16), "fsdp", scatter_dimension=3, tiled=True
    ).astype(jnp.float32)
    hidden = (jax.nn.silu(summed[:, :, 0]) * summed[:, :, 1]).astype(jnp.bfloat16)
    result = jnp.einsum(
        "ksh,khd->ksd",
        lax.all_gather(hidden, "fsdp", axis=2, tiled=True),
        down_rows,
        preferred_element_type=jnp.float32,
    )
    output = result.astype(jnp.bfloat16)
    served = output[None, :, None]
    served_rows = served[0, :, 0]
    back_view = served_rows.reshape(per_owner, owners, groups, capacity, served_rows.shape[2])
    returned = lax.all_to_all(
        lax.all_to_all(back_view, "fsdp", split_axis=2, concat_axis=4, tiled=True),
        "expert",
        split_axis=1,
        concat_axis=0,
        tiled=True,
    )
    gathered = returned.reshape(experts * capacity, width).astype(jnp.float32)
    mixed = jnp.dot(
        blend_table, gathered, precision=lax.Precision.HIGHEST, preferred_element_type=jnp.float32
    )
    return (element_got[0], mixed.astype(jnp.bfloat16))


def solution(mesh):
    return jax.shard_map(
        body,
        mesh=mesh,
        in_specs=(
            P(("fsdp", "expert"), None),
            P(None, None, "expert", "fsdp"),
            P(None, None, "expert", "fsdp"),
            P(("fsdp", "expert"), None),
            P(("fsdp", "expert"), None),
        ),
        out_specs=(P("expert", None, None, "fsdp"), P(("fsdp", "expert"), None)),
        check_vma=False,
    )
```

profile of v0, /device:TPU:1, one launch (start us, length us, event | category | flops | bytes accessed | tf_op | source)
XLA Modules:
  0.0 470.8 jit_solution(17510148527857416157)
XLA Ops:
  10.3 2.0 convolution_convert_fusion
  12.3 2.7 reshape.49
  15.0 9.7 %copy.89 = bf16[32,2,1,4,4096]{0,3,2,1,4:T(4,128)(2,1)} copy(bf16[32,2,1,4,4096]{4,3,1,0,2:T(4,128)(2,1)S(1)} %reshape.49) | data formatting | bytes 4194304 | tf_op jit(solution)/shard_map/reshape | solution.py:49
  24.7 11.3 %reshape.55 = bf16[8,2,65536]{2,1,0:T(2,128)(2,1)} reshape(bf16[4096,2,1,4,32]{4,3,2,1,0:T(4,128)(2,1)} %bitcast.70) | data formatting | bytes 4194304
  35.9 6.7 %all-to-all-start.1 = ((bf16[8,2,65536]{2,1,0:T(2,128)(2,1)}), bf16[8,2,65536]{2,1,0:T(2,128)(2,1)S(1)}, u32[]{:S(2)}, u32[]{:S(2)}) async-start(bf16[8,2,65536]{2,1,0:T(2,128)(2,1)} %reshape.55), calls=%async_computation.1 | async-start | bytes 4194304 | tf_op jit(solution)/shard_map/all_to_all | solution.py:55
  43.5 1.7 reshape.57
  45.2 23.7 %all-to-all-done.1 = bf16[8,2,65536]{2,1,0:T(2,128)(2,1)S(1)} async-done(((bf16[8,2,65536]{2,1,0:T(2,128)(2,1)}), bf16[8,2,65536]{2,1,0:T(2,128)(2,1)S(1)}, u32[]{:S(2)}, u32[]{:S(2)}) %all-to-all-start.1) | async-done | bytes 2097184 | tf_op jit(solution)/shard_map/all_to_all | solution.py:55
  68.9 10.3 %all-to-all-start.3 = ((bf16[32,2,1152]{2,1,0:T(2,128)(2,1)}), bf16[32,2,1152]{2,1,0:T(2,128)(2,1)S(1)}, u32[]{:S(2)}, u32[]{:S(2)}) async-start(bf16[32,2,1152]{2,1,0:T(2,128)(2,1)} %reshape.57), calls=%async_computation.3 | async-start | bytes 294912 | tf_op jit(solution)/shard_map/all_to_all | solution.py:52
  79.2 6.6 %reshape.56 = bf16[4096,2,1,4,32]{4,3,2,1,0:T(4,128)(2,1)} reshape(bf16[8,2,65536]{2,1,0:T(2,128)(2,1)S(1)} %all-to-all-done.1) | data formatting | bytes 4194304
  85.7 12.0 %copy.90 = bf16[32,2,1,8,4,512]{5,4,3,1,0,2:T(4,128)(2,1)S(1)} copy(bf16[32,2,1,8,4,512]{0,4,1,5,3,2:T(4,128)(2,1)} %bitcast.71) | data formatting | bytes 4194304 | tf_op jit(solution)/shard_map/all_to_all | solution.py:55
  97.7 2.0 all_to_all.76
  100.4 9.2 %all-to-all-start.2 = ((bf16[32,2,1,32,512]{4,3,1,2,0:T(8,128)(2,1)}), bf16[32,2,1,32,512]{4,3,1,2,0:T(8,128)(2,1)S(1)}, u32[]{:S(2)}, u32[]{:S(2)}) async-start(bf16[32,2,1,32,512]{4,3,1,2,0:T(8,128)(2,1)} %all_to_all.76), calls=%async_computation.2 | async-start | bytes 4194304 | tf_op jit(solution)/shard_map/all_to_all | solution.py:54
  109.6 10.6 %copy.83 = bf16[64,3,24,512]{0,3,2,1:T(8,128)(2,1)} copy(bf16[64,3,24,512]{3,2,1,0:T(8,128)(2,1)} %param.6) | data formatting | bytes 9437184 | tf_op args[1]
  120.2 23.1 %multiply_convert_fusion = bf16[64,3,24,512]{0,3,2,1:T(8,128)(2,1)} fusion(bf16[64,3,24,512]{0,3,2,1:T(8,128)(2,1)} %copy.83, bf16[64,3,24,16]{0,3,2,1:T(8,128)(2,1)S(1)} %exponential_convert_fusion), kind=kLoop, calls=%fused_computation | loop fusion | flops 63700992 | bytes 9584640 | tf_op jit(solution)/shard_map/convert_element_type | solution.py:19
  143.3 11.3 %copy.84 = bf16[64,3,24,512]{3,2,1,0:T(8,128)(2,1)} copy(bf16[64,3,24,512]{0,3,2,1:T(8,128)(2,1)} %multiply_convert_fusion) | data formatting | bytes 9437184 | tf_op jit(solution)/shard_map/convert_element_type | solution.py:19
  154.6 2.8 all-to-all-done.2
  157.4 7.1 %all-to-all-start = ((bf16[32,2,3,24,512]{4,3,2,1,0:T(8,128)(2,1)}), bf16[32,2,3,24,512]{4,3,2,1,0:T(8,128)(2,1)}, u32[]{:S(2)}, u32[]{:S(2)}) async-start(bf16[32,2,3,24,512]{4,3,2,1,0:T(8,128)(2,1)} %bitcast.74), calls=%async_computation | async-start | bytes 9437184 | tf_op jit(solution)/shard_map/all_to_all | solution.py:51
  167.3 2.5 broadcast_in_dim.5
  169.9 6.7 %copy.94 = bf16[2,3,768,512]{3,2,1,0:T(8,128)(2,1)} copy(bf16[2,3,768,512]{2,3,1,0:T(8,128)(2,1)} %bitcast.77) | data formatting | bytes 9437184 | tf_op jit(solution)/shard_map/reshape | solution.py:61
  178.1 89.8 %all-to-all-done = bf16[32,2,3,24,512]{4,3,2,1,0:T(8,128)(2,1)} async-done(((bf16[32,2,3,24,512]{4,3,2,1,0:T(8,128)(2,1)}), bf16[32,2,3,24,512]{4,3,2,1,0:T(8,128)(2,1)}, u32[]{:S(2)}, u32[]{:S(2)}) %all-to-all-start) | async-done | bytes 4718624 | tf_op jit(solution)/shard_map/all_to_all | solution.py:51
  268.0 2.9 copy.85
  274.0 2.2 copy-done.3
  276.2 5.4 %convolution_convert_fusion.2 = bf16[2,1024,2,768]{1,3,2,0:T(8,128)(2,1)} fusion(bf16[2,1024,512,1]{2,1,3,0:T(8,128)(2,1)S(1)} %bitcast.82, bf16[2,3,768,512]{3,2,1,0:T(8,128)(2,1)S(1)} %mul.64), kind=kOutput, calls=%fused_computation.13 | convolution fusion | flops 3224371200 | bytes 11534336 | tf_op jit(solution)/shard_map/ksd,kghd->ksgh/dot_general | solution.py:65
  281.7 43.4 %reduce-scatter.2.cloned.1.call-done = bf16[2,1024,2,96]{1,3,2,0:T(8,128)(2,1)} async-done(((bf16[2,1024,2,768]{1,3,2,0:T(8,128)(2,1)}), bf16[2,1024,2,96]{1,3,2,0:T(8,128)(2,1)}) %reduce-scatter.2.cloned.1.call-update) | async-done | bytes 786448 | tf_op jit(solution)/shard_map/reduce_scatter | solution.py:68
  327.4 31.1 %all-gather.2.cloned.1.call-done = bf16[2,1024,768]{1,2,0:T(8,128)(2,1)} async-done(((bf16[2,1024,96]{1,2,0:T(8,128)(2,1)}), bf16[2,1024,768]{1,2,0:T(8,128)(2,1)}) %all-gather.2.cloned.1.call-update) | async-done | bytes 3145744 | tf_op jit(solution)/shard_map/all_gather | solution.py:74
  358.5 5.5 %convolution_convert_fusion.3 = bf16[2,1024,512]{2,1,0:T(8,128)(2,1)} fusion(bf16[2,1024,768]{1,2,0:T(8,128)(2,1)} %all-gather.2.cloned.1.call-done, bf16[2,3,768,512]{3,2,1,0:T(8,128)(2,1)} %copy-done.3), kind=kOutput, calls=%fused_computation.15 | convolution fusion | flops 1611661312 | bytes 6815744 | tf_op jit(solution)/shard_map/ksh,khd->ksd/dot_general | solution.py:72
  364.0 2.5 reshape_squeeze_broadcast_in_dim.3
  367.5 29.2 %all_to_all.96 = bf16[2,32,8,4,512]{4,3,1,0,2:T(4,128)(2,1)S(1)} all-to-all(bf16[2,32,8,4,512]{4,3,1,0,2:T(4,128)(2,1)S(1)} %copy.96), channel_id=1, replica_groups=mesh['fsdp'=8,'expert'=32] {'fsdp'}, dimensions={2} | all-to-all | bytes 4194304 | tf_op jit(solution)/shard_map/all_to_all | solution.py:83
  396.7 2.2 copy.100
  399.0 2.8 reshape.54
  401.7 58.1 %all_to_all.97 = bf16[2,32,1,4,4096]{4,3,0,2,1:T(4,128)(2,1)} all-to-all(bf16[2,32,1,4,4096]{4,3,0,2,1:T(4,128)(2,1)} %reshape.54), channel_id=1, replica_groups=mesh['fsdp'=8,'expert'=32] {'expert'}, dimensions={1} | all-to-all | bytes 4194304 | tf_op jit(solution)/shard_map/all_to_all | solution.py:82
  459.8 2.5 reshape.52
  (48 shorter events, 16.8 us)
Async XLA Ops:
  7.2 3.1 copy-start
  24.7 18.0 %copy-start.7 = (s32[64,3,24,16]{0,3,2,1:T(8,128)S(1)}, s32[64,3,24,16]{0,3,2,1:T(8,128)}, u32[]{:S(2)}) copy-start(s32[64,3,24,16]{0,3,2,1:T(8,128)} %param.7) | copy-start | bytes 884740
  35.9 32.9 %all-to-all-start.1 = ((bf16[8,2,65536]{2,1,0:T(2,128)(2,1)}), bf16[8,2,65536]{2,1,0:T(2,128)(2,1)S(1)}, u32[]{:S(2)}, u32[]{:S(2)}) async-start(bf16[8,2,65536]{2,1,0:T(2,128)(2,1)} %reshape.55), calls=%async_computation.1 | async-start | bytes 4194304 | tf_op jit(solution)/shard_map/all_to_all | solution.py:55
  68.9 30.8 %all-to-all-start.3 = ((bf16[32,2,1152]{2,1,0:T(2,128)(2,1)}), bf16[32,2,1152]{2,1,0:T(2,128)(2,1)S(1)}, u32[]{:S(2)}, u32[]{:S(2)}) async-start(bf16[32,2,1152]{2,1,0:T(2,128)(2,1)} %reshape.57), calls=%async_computation.3 | async-start | bytes 294912 | tf_op jit(solution)/shard_map/all_to_all | solution.py:52
  99.7 0.7 copy-start.5
  100.4 57.0 %all-to-all-start.2 = ((bf16[32,2,1,32,512]{4,3,1,2,0:T(8,128)(2,1)}), bf16[32,2,1,32,512]{4,3,1,2,0:T(8,128)(2,1)S(1)}, u32[]{:S(2)}, u32[]{:S(2)}) async-start(bf16[32,2,1,32,512]{4,3,1,2,0:T(8,128)(2,1)} %all_to_all.76), calls=%async_computation.2 | async-start | bytes 4194304 | tf_op jit(solution)/shard_map/all_to_all | solution.py:54
  157.4 7.2 %copy-start.6 = (bf16[32,2,1152]{2,1,0:T(2,128)(2,1)S(1)}, bf16[32,2,1152]{2,1,0:T(2,128)(2,1)}, u32[]{:S(2)}) copy-start(bf16[32,2,1152]{2,1,0:T(2,128)(2,1)} %copy-done.5) | copy-start | bytes 442372
  157.4 110.5 %all-to-all-start = ((bf16[32,2,3,24,512]{4,3,2,1,0:T(8,128)(2,1)}), bf16[32,2,3,24,512]{4,3,2,1,0:T(8,128)(2,1)}, u32[]{:S(2)}, u32[]{:S(2)}) async-start(bf16[32,2,3,24,512]{4,3,2,1,0:T(8,128)(2,1)} %bitcast.74), calls=%async_computation | async-start | bytes 9437184 | tf_op jit(solution)/shard_map/all_to_all | solution.py:51
  164.5 160.5 %reduce-scatter.2.cloned.1.call-start = ((), (), s32[]{:S(2)}) async-start(), calls=%async_computation.7 | async-start | bytes 7077888 | tf_op jit(solution)/shard_map/reduce_scatter | solution.py:68
  176.6 94.3 %slice-start = ((s8[4718592]{0:T(1024)(128)(4,1)}), s8[524288]{0:T(1024)(128)(4,1)S(1)}, s32[]{:S(2)}) async-start(s8[4718592]{0:T(1024)(128)(4,1)} %bitcast.75), calls=%async_computation.9 | async-start | bytes 1048576
  268.0 3.6 slice-start.1
  270.9 3.1 copy-start.2
  271.6 4.7 copy-start.4
  274.0 2.2 copy-start.3
  281.6 76.9 %all-gather.2.cloned.1.call-start = ((), (), s32[]{:S(2)}) async-start(), calls=%async_computation.8 | async-start | bytes 3538944 | tf_op jit(solution)/shard_map/all_gather | solution.py:74
  399.0 65.0 %copy-start.1 = (bf16[16,4096]{1,0:T(8,128)(2,1)S(1)}, bf16[16,4096]{1,0:T(8,128)(2,1)}, u32[]{:S(2)}) copy-start(bf16[16,4096]{1,0:T(8,128)(2,1)} %param.5) | copy-start | bytes 393220
Sparse Core Ops, SparseCore 0:
  281.7 43.2 reduce-scatter.1
  327.5 30.9 all-gather.1
where the time goes:
time: 474 us; the launch traced here: 471 us
  waiting for transfers between devices  191 us (40%)
  local copies, waits for them, and re-layouts  101 us (21%)
  blocking collectives  87.3 us (18%)
  starting transfers between devices  33.4 us (7%)
  other arithmetic  29 us (6%)
  matrix products  14.5 us (3%)
  between operations  14.3 us (3%)
    all_to_all x1, waiting for transfers between devices, body(): lax.all_to_all(element_view, 'expert', split_axis=0, concat_axis=3, tiled...  89.8 us
    all_to_all x1, blocking collectives, body(): lax.all_to_all(lax.all_to_all(back_view, 'fsdp', split_axis=2, concat_axi...  58.1 us
    reduce_scatter x1, waiting for transfers between devices, body(): lax.psum_scatter(partial_value.astype(jnp.bfloat16), 'fsdp', scatter_dime...  43.4 us
    unnamed x26, local copies, waits for them, and re-layouts  36.4 us
    all_gather x1, waiting for transfers between devices, body(): lax.all_gather(hidden, 'fsdp', axis=2, tiled=True)  31.1 us
    all_to_all x1, blocking collectives, body(): lax.all_to_all(back_view, 'fsdp', split_axis=2, concat_axis=4, tiled=True)  29.2 us
    all_to_all x1, waiting for transfers between devices, body(): lax.all_to_all(packed_view, 'fsdp', split_axis=4, concat_axis=3, tiled=True)  23.7 us
    convert_element_type x1, other arithmetic, to_grid(): return (jnp.sign(clipped) * level.astype(jnp.float32)).astype(jnp.bfloat16)  23.1 us
  transfers between devices with their start and end apart: 6, of which 5 were waited for; matrix products, arithmetic and copies ran while one was open for 17% of the time, Pallas kernels for 0%

commit v1 on v0

v1 whole, which is shorter than its diff:
```python
import functools
import jax
import jax.numpy as jnp
from jax import lax
from jax.experimental import pallas as pl
from jax.experimental.pallas import tpu as pltpu
from jax.sharding import PartitionSpec as P

BLOCK = 32
MESH = pl.DeviceIdType.MESH


def encode_send(rows, inv, scl, out, s_out, buf, enc, ssend, load_sem, send_sem, recv_sem, own_sem, sc_send, sc_recv, sc_own):
    me = lax.axis_index("expert")
    n = 32
    barrier = pltpu.get_barrier_semaphore()

    def load(ph):
        k, p = PHASES[ph]
        return pltpu.make_async_copy(rows.at[:, k, p], buf.at[ph % 2], load_sem.at[ph % 2])

    load(0).start()

    def greet(j, c):
        peer = lax.rem(me + j, n)
        pl.semaphore_signal(barrier, inc=1, device_id={"expert": peer}, device_id_type=MESH)
        return c

    lax.fori_loop(1, n, greet, 0)

    def scale_copy(j):
        peer = lax.rem(me + j, n)
        return pltpu.make_async_remote_copy(
            src_ref=scl.at[peer], dst_ref=s_out.at[me], send_sem=sc_send, recv_sem=sc_recv,
            device_id={"expert": peer}, device_id_type=MESH)

    def elem_copy(ph, j):
        k, p = PHASES[ph]
        peer = lax.rem(me + j, n)
        return pltpu.make_async_remote_copy(
            src_ref=enc.at[ph, peer], dst_ref=out.at[k, p, me], send_sem=send_sem.at[ph], recv_sem=recv_sem.at[ph],
            device_id={"expert": peer}, device_id_type=MESH)

    for ph in range(6):
        k, p = PHASES[ph]
        kp = k * 3 + p
        load(ph).wait()
        if ph + 1 < 6:
            load(ph + 1).start()
        lane = lax.broadcasted_iota(jnp.int32, (128, 512), 0)
        feat = lax.broadcasted_iota(jnp.int32, (128, 512), 1)
        pick = (lane == kp * 16 + feat // BLOCK).astype(jnp.bfloat16)

        def enc_one(o, c):
            wide = jnp.dot(inv[o], pick, preferred_element_type=jnp.float32)
            x = buf[ph % 2, o].astype(jnp.float32) * wide
            x = jnp.minimum(jnp.maximum(x, -6.0), 6.0)
            a = jnp.abs(x)
            magic = jnp.where(a < 2.0, 0.5 * 12582912.0, jnp.where(a < 4.0, 12582912.0, 2.0 * 12582912.0))
            enc[ph, o] = ((x + magic) - magic).astype(jnp.bfloat16)
            return c

        lax.fori_loop(0, n, enc_one, 0)
        if ph == 0:
            pl.semaphore_wait(barrier, n - 1)

            def sc_one(j, c):
                scale_copy(j).start()
                return c

            lax.fori_loop(1, n, sc_one, 0)
            pltpu.make_async_copy(scl.at[me], s_out.at[me], sc_own).start()

        def send_one(j, c):
            elem_copy(ph, j).start()
            return c

        lax.fori_loop(1, n, send_one, 0)
        pltpu.make_async_copy(enc.at[ph, me], out.at[k, p, me], own_sem.at[ph]).start()

    for ph in range(6):
        k, p = PHASES[ph]
        pltpu.make_async_copy(enc.at[ph, me], out.at[k, p, me], own_sem.at[ph]).wait()
        many = pl.ds(0, n - 1)
        pltpu.make_async_copy(enc.at[ph, many], out.at[k, p, many], send_sem.at[ph]).wait()
        pltpu.make_async_copy(enc.at[ph, many], out.at[k, p, many], recv_sem.at[ph]).wait()
    pltpu.make_async_copy(scl.at[me], s_out.at[me], sc_own).wait()
    many = pl.ds(0, n - 1)
    pltpu.make_async_copy(scl.at[many], s_out.at[many], sc_send).wait()
    pltpu.make_async_copy(scl.at[many], s_out.at[many], sc_recv).wait()


PHASES = [(0, 0), (0, 1), (1, 0), (1, 1), (0, 2), (1, 2)]


def dispatch(rows, inv, scl):
    vm = pl.BlockSpec(memory_space=pltpu.VMEM)
    hbm = pl.BlockSpec(memory_space=pl.ANY)
    return pl.pallas_call(
        encode_send,
        out_shape=(jax.ShapeDtypeStruct((2, 3, 32, 24, 512), jnp.bfloat16), jax.ShapeDtypeStruct((32, 24, 128), jnp.bfloat16)),
        in_specs=[hbm, vm, hbm],
        out_specs=(hbm, hbm),
        scratch_shapes=[
            pltpu.VMEM((2, 32, 24, 512), jnp.bfloat16),
            pltpu.VMEM((6, 32, 24, 512), jnp.bfloat16),
            pltpu.VMEM((8, 128), jnp.bfloat16),
            pltpu.SemaphoreType.DMA((2,)),
            pltpu.SemaphoreType.DMA((6,)),
            pltpu.SemaphoreType.DMA((6,)),
            pltpu.SemaphoreType.DMA((6,)),
            pltpu.SemaphoreType.DMA,
            pltpu.SemaphoreType.DMA,
            pltpu.SemaphoreType.DMA,
        ],
        compiler_params=pltpu.CompilerParams(collective_id=1, has_side_effects=True, vmem_limit_bytes=40 << 20),
        cost_estimate=pl.CostEstimate(flops=2 * 4608 * 128 * 512, bytes_accessed=14 << 20, transcendentals=0),
        name="encode_send",
    )(rows, inv, scl)


def body(tokens, learner_rows, exponents, expert_ids, route_probs):
    exps = exponents.reshape(32, 2, 3, 24, 16).transpose(0, 3, 1, 2, 4).reshape(32, 24, 96).astype(jnp.float32)
    pad = ((0, 0), (0, 0), (0, 32))
    scl = jnp.pad(jnp.exp2(exps), pad).astype(jnp.bfloat16)
    inv = jnp.pad(jnp.exp2(-exps), pad).astype(jnp.bfloat16)
    el, sc = dispatch(learner_rows.reshape(32, 2, 3, 24, 512), inv, scl)
    elements = el.reshape(2, 3, 768, 512)
    spread = lax.all_to_all(tokens.reshape(16, 8, 512), "fsdp", split_axis=1, concat_axis=0, tiled=True).reshape(128, 512)
    held = lax.all_gather(spread, "expert", axis=0, tiled=True)
    meta = jnp.concatenate([expert_ids.astype(jnp.float32).T, route_probs.T], axis=0)
    meta = lax.all_gather(meta, "fsdp", axis=1, tiled=True)
    meta = lax.all_gather(meta, "expert", axis=0, tiled=False)
    ids = meta[:, :8].astype(jnp.int32)
    probs = meta[:, 8:]
    share = probs / jnp.sum(probs, axis=1, keepdims=True)
    mine = lax.axis_index("expert") * 2 + jnp.arange(2, dtype=jnp.int32)
    hit = (ids[:, None] == mine[None, :, None, None])
    member = jnp.any(hit, axis=2)
    weight = jnp.sum(jnp.where(hit, share[:, None], 0.0), axis=2)
    lane = jnp.arange(128, dtype=jnp.int32)
    tri = ((lane[:, None] // 16 == lane[None, :] // 16) & (lane[:, None] < lane[None, :])).astype(jnp.float32)
    pos = jnp.einsum("gkt,tu->gku", member.astype(jnp.float32), tri).astype(jnp.int32)
    code = jnp.where(member, (lane // 16) * 4 + pos, -1)
    onehot = code[:, :, None, :] == jnp.arange(32, dtype=jnp.int32)[None, None, :, None]
    slots = jnp.einsum("gkst,gtd->kgsd", onehot.astype(jnp.bfloat16), held.reshape(32, 128, 512), preferred_element_type=jnp.float32).astype(jnp.bfloat16).reshape(2, 1024, 512)
    sc = sc.reshape(768, 128)
    scw = jnp.stack([jnp.repeat(sc[:, i * 16:(i + 1) * 16], BLOCK, axis=1) for i in range(6)]).reshape(2, 3, 768, 512)
    weights = elements * scw
    part = jnp.einsum("ksd,kghd->ksgh", slots, weights[:, 0:2], preferred_element_type=jnp.float32).astype(jnp.bfloat16)
    summed = lax.psum_scatter(part, "fsdp", scatter_dimension=1, tiled=True).astype(jnp.float32)
    hidden = (jax.nn.silu(summed[:, :, 0]) * summed[:, :, 1]).astype(jnp.bfloat16)
    hidden = lax.all_gather(hidden, "fsdp", axis=1, tiled=True)
    outs = jnp.einsum("ksh,khd->ksd", hidden, weights[:, 2], preferred_element_type=jnp.float32).astype(jnp.bfloat16)
    blend = onehot.astype(jnp.float32) * weight[:, :, None, :]
    outs_g = outs.reshape(2, 32, 32, 512).transpose(1, 0, 2, 3).reshape(32, 64, 512)
    hi = blend.astype(jnp.bfloat16)
    lo = (blend - hi.astype(jnp.float32)).astype(jnp.bfloat16)
    two = jnp.concatenate([hi.reshape(32, 64, 128), lo.reshape(32, 64, 128)], axis=1)
    mixed = jnp.einsum("gst,gsd->gtd", two, jnp.concatenate([outs_g, outs_g], axis=1), preferred_element_type=jnp.float32)
    mixed = mixed.astype(jnp.bfloat16)
    mine_mixed = lax.psum_scatter(mixed.reshape(4096, 512), "expert", scatter_dimension=0, tiled=True)
    mixed_out = lax.all_to_all(mine_mixed, "fsdp", split_axis=0, concat_axis=1, tiled=True)
    return elements, mixed_out


def solution(mesh):
    return jax.shard_map(
        body,
        mesh=mesh,
        in_specs=(
            P(("fsdp", "expert"), None),
            P(None, None, "expert", "fsdp"),
            P(None, None, "expert", "fsdp"),
            P(("fsdp", "expert"), None),
            P(("fsdp", "expert"), None),
        ),
        out_specs=(P("expert", None, None, "fsdp"), P(("fsdp", "expert"), None)),
        check_vma=False,
    )
```

time: 474 us -> 591 us (1.25)
  Pallas kernels: 0 us -> 140 us
  waiting for transfers between devices: 191 us -> 299 us
  local copies, waits for them, and re-layouts: 101 us -> 31.7 us
  blocking collectives: 87.3 us -> 64.1 us
  starting transfers between devices: 33.4 us -> 10.5 us
  other arithmetic: 29 us -> 14.4 us
    reduce_scatter x1 -> x2, waiting for transfers between devices: 43.4 us -> 270 us  [the longest x1 218 us: body(): lax.psum_scatter(mixed.reshape(4096, 512), 'expert', scatter_dimension=0,...]
    pallas_call x0 -> x1, Pallas kernels: none -> 140 us  [dispatch(): pl.pallas_call(encode_send, out_shape=(jax.ShapeDtypeStruct((2, 3, 32, 24...]
    all_to_all x4 -> x1, waiting for transfers between devices: 116 us -> 5.24 us  [body(): lax.all_to_all(mine_mixed, 'fsdp', split_axis=0, concat_axis=1, tiled=True)]
    all_to_all x2 -> x1, blocking collectives: 87.3 us -> 11.5 us  [body(): lax.all_to_all(tokens.reshape(16, 8, 512), 'fsdp', split_axis=1, concat_a...]
    all_gather x0 -> x2, blocking collectives: none -> 52.6 us  [the longest x1 38.2 us: body(): meta = lax.all_gather(meta, 'expert', axis=0, tiled=False)]
    all_to_all x8 -> x1, local copies, waits for them, and re-layouts: 23.8 us -> 0.66 us  [body(): lax.all_to_all(mine_mixed, 'fsdp', split_axis=0, concat_axis=1, tiled=True)]
    all_to_all x4 -> x1, starting transfers between devices: 33.3 us -> 10.2 us  [body(): lax.all_to_all(mine_mixed, 'fsdp', split_axis=0, concat_axis=1, tiled=True)]
    reshape x4 -> x1, local copies, waits for them, and re-layouts: 21.7 us -> 0.91 us  [body(): tokens.reshape(16, 8, 512)]
  transfers between devices with their start and end apart: 6 -> 5, of which waited for: 5 -> 4; matrix products, arithmetic and copies ran while one was open for 17% -> 5% of each run, Pallas kernels for 0% -> 24%
where the time goes in v1:
time: 591 us; the launch traced here: 590 us
  waiting for transfers between devices  299 us (51%)
  Pallas kernels  140 us (24%)
  blocking collectives  64.1 us (11%)
  local copies, waits for them, and re-layouts  31.7 us (5%)
  matrix products  15.7 us (3%)
  other arithmetic  14.4 us (2%)
  between operations  14 us (2%)
  starting transfers between devices  10.5 us (2%)
    reduce_scatter x1, waiting for transfers between devices, body(): lax.psum_scatter(mixed.reshape(4096, 512), 'expert', scatter_dimension=0,...  218 us
    pallas_call x1, Pallas kernels, dispatch(): pl.pallas_call(encode_send, out_shape=(jax.ShapeDtypeStruct((2, 3, 32, 24...  140 us
    reduce_scatter x1, waiting for transfers between devices, body(): lax.psum_scatter(part, 'fsdp', scatter_dimension=1, tiled=True)  52 us
    all_gather x1, blocking collectives, body(): meta = lax.all_gather(meta, 'expert', axis=0, tiled=False)  38.2 us
    all_gather x1, waiting for transfers between devices, body(): hidden = lax.all_gather(hidden, 'fsdp', axis=1, tiled=True)  24.3 us
    unnamed x22, local copies, waits for them, and re-layouts  15.8 us
    all_gather x1, blocking collectives, body(): meta = lax.all_gather(meta, 'fsdp', axis=1, tiled=True)  14.3 us
  transfers between devices with their start and end apart: 5, of which 4 were waited for; matrix products, arithmetic and copies ran while one was open for 5% of the time, Pallas kernels for 24%

profile of v1, /device:TPU:1, one launch (start us, length us, event | category | flops | bytes accessed | tf_op | source)
XLA Modules:
  0.0 590.1 jit_solution(10016610595012160724)
XLA Ops:
  7.2 0.9 copy.146
  8.1 11.5 %all_to_all.34 = bf16[16,8,512]{2,0,1:T(8,128)(2,1)} all-to-all(bf16[16,8,512]{2,0,1:T(8,128)(2,1)S(1)} %bitcast.101), channel_id=1, replica_groups=mesh['fsdp'=8,'expert'=32] {'fsdp'}, dimensions={1} | all-to-all | bytes 262144 | tf_op jit(solution)/shard_map/all_to_all | solution.py:129
  19.7 1.2 exponential_convert_fusion.1
  23.1 2.3 copy-done.1
  25.4 140.2 %encode_send.1 = (bf16[2,3,32,24,512]{4,3,2,1,0:T(8,128)(2,1)S(1)}, bf16[32,24,128]{2,1,0:T(8,128)(2,1)S(1)}) custom-call(bf16[32,2,3,24,512]{4,3,2,1,0:T(8,128)(2,1)S(1)} %bitcast.80, bf16[32,24,128]{2,1,0:T(8,128)(2,1)S(1)} %pad.9.inv, bf16[32,24,128]{2,1,0:T(8,128)(2,1)S(1)} %pad.10.scl), custom_call_target="tpu_custom_call" | custom-call | flops 603979776 | bytes 14680064 | tf_op jit(solution)/shard_map/encode_send/pallas_call | solution.py:99
  165.7 2.1 copy-done
  168.9 0.9 constant_dynamic-update-slice_fusion.5
  169.9 0.9 constant_dynamic-update-slice_fusion.4
  170.9 0.9 constant_dynamic-update-slice_fusion.3
  171.9 0.9 constant_dynamic-update-slice_fusion.2
  172.9 0.9 constant_dynamic-update-slice_fusion.1
  173.9 0.9 constant_dynamic-update-slice_fusion
  174.8 6.7 %copy.130 = bf16[6,768,512]{2,1,0:T(8,128)(2,1)} copy(bf16[6,768,512]{1,2,0:T(8,128)(2,1)} %constant_dynamic-update-slice_fusion) | data formatting | bytes 9437184 | tf_op jit(solution)/shard_map/stack | solution.py:148
  181.6 14.3 %all_gather.15 = f32[16,128]{0,1:T(8,128)S(1)} all-gather(f32[16,16]{0,1:T(8,128)S(1)} %copy.115), channel_id=1, replica_groups=mesh['fsdp'=8,'expert'=32] {'fsdp'}, dimensions={1}, use_global_device_ids=true | all-gather | bytes 9216 | tf_op jit(solution)/shard_map/all_gather | solution.py:132
  196.0 38.2 %all-gather = f32[512,128]{1,0:T(8,128)S(1)} all-gather(f32[16,128]{1,0:T(8,128)S(1)} %copy.116), channel_id=2, replica_groups=mesh['fsdp'=8,'expert'=32] {'expert'}, dimensions={0}, use_global_device_ids=true | all-gather | bytes 270336 | tf_op jit(solution)/shard_map/all_gather | solution.py:133
  235.3 6.4 %bitcast_multiply_fusion = bf16[2,3,768,512]{3,2,1,0:T(8,128)(2,1)} fusion(bf16[2,3,768,512]{3,2,1,0:T(8,128)(2,1)} %bitcast.81, bf16[2,3,32,24,512]{4,3,2,1,0:T(8,128)(2,1)} %copy-done), kind=kLoop, calls=%fused_computation.61 | loop fusion | flops 2359296 | bytes 14155776 | tf_op jit(solution)/shard_map/mul | solution.py:149
  241.8 3.0 convert_bitcast_fusion
  245.4 5.4 convolution_convert_fusion
  250.8 52.0 %reduce-scatter.3.cloned.1.call-done = bf16[2,128,2,768]{3,1,2,0:T(8,128)(2,1)} async-done(((bf16[2,1024,2,768]{3,1,2,0:T(8,128)(2,1)}), bf16[2,128,2,768]{3,1,2,0:T(8,128)(2,1)}) %reduce-scatter.3.cloned.1.call-update) | async-done | bytes 786448 | tf_op jit(solution)/shard_map/reduce_scatter | solution.py:151
  302.9 1.3 convert_element_type.68
  304.1 1.0 fusion.15
  306.3 2.0 copy.121
  308.4 2.0 fusion.13
  310.6 1.4 subtract_convert_fusion
  312.0 24.3 %all-gather.6.cloned.1.call-done = bf16[2,1024,768]{2,1,0:T(8,128)(2,1)} async-done(((bf16[2,128,768]{2,1,0:T(8,128)(2,1)}), bf16[2,1024,768]{2,1,0:T(8,128)(2,1)}) %all-gather.6.cloned.1.call-update) | async-done | bytes 3145744 | tf_op jit(solution)/shard_map/all_gather | solution.py:153
  336.3 4.1 convolution_convert_fusion.1
  340.6 1.1 copy-done.3
  341.7 2.9 fusion.5
  344.6 217.8 %reduce-scatter.5.cloned.1.call-done = bf16[128,512]{1,0:T(8,128)(2,1)} async-done(((bf16[4096,512]{1,0:T(8,128)(2,1)}), bf16[128,512]{1,0:T(8,128)(2,1)}) %reduce-scatter.5.cloned.1.call-update) | async-done | bytes 131088 | tf_op jit(solution)/shard_map/reduce_scatter | solution.py:162
  562.4 10.2 %all-to-all-start.1 = ((bf16[8,16,512]{2,1,0:T(8,128)(2,1)}), bf16[8,16,512]{2,1,0:T(8,128)(2,1)S(1)}, u32[]{:S(2)}, u32[]{:S(2)}) async-start(bf16[8,16,512]{2,1,0:T(8,128)(2,1)} %bitcast.104), calls=%async_computation.3 | async-start | bytes 262144 | tf_op jit(solution)/shard_map/all_to_all | solution.py:163
  572.6 5.2 all-to-all-done.1
  578.5 5.1 copy.153
  (61 shorter events, 7.6 us)
Async XLA Ops:
  7.2 234.6 %all-gather.4.cloned.1.call-start = ((), (), s32[]{:S(2)}) async-start(), calls=%async_computation.4 | async-start | bytes 4325376 | tf_op jit(solution)/shard_map/all_gather | solution.py:130
  19.7 283.2 %reduce-scatter.3.cloned.1.call-start = ((), (), s32[]{:S(2)}) async-start(), calls=%async_computation.5 | async-start | bytes 7077888 | tf_op jit(solution)/shard_map/reduce_scatter | solution.py:151
  23.1 2.3 copy-start.1
  165.7 2.1 copy-start
  174.8 6.7 %copy-start.4 = (s32[16,8]{0,1:T(8,128)S(1)}, s32[16,8]{0,1:T(8,128)}, u32[]{:S(2)}) copy-start(s32[16,8]{0,1:T(8,128)} %param.8) | copy-start | bytes 1540
  174.8 6.7 %copy-start.5 = (f32[16,8]{0,1:T(8,128)S(1)}, f32[16,8]{0,1:T(8,128)}, u32[]{:S(2)}) copy-start(f32[16,8]{0,1:T(8,128)} %param.9) | copy-start | bytes 1540
  241.8 3.4 slice-start
  241.8 3.6 slice-start.1
  250.8 85.5 %all-gather.6.cloned.1.call-start = ((), (), s32[]{:S(2)}) async-start(), calls=%async_computation.6 | async-start | bytes 3538944 | tf_op jit(solution)/shard_map/all_gather | solution.py:153
  305.2 257.2 %reduce-scatter.5.cloned.1.call-start = ((), (), s32[]{:S(2)}) async-start(), calls=%async_computation.7 | async-start | bytes 4325376 | tf_op jit(solution)/shard_map/reduce_scatter | solution.py:162
  308.4 2.2 copy-start.2
  340.4 1.2 copy-start.3
  562.4 15.4 %all-to-all-start.1 = ((bf16[8,16,512]{2,1,0:T(8,128)(2,1)}), bf16[8,16,512]{2,1,0:T(8,128)(2,1)S(1)}, u32[]{:S(2)}, u32[]{:S(2)}) async-start(bf16[8,16,512]{2,1,0:T(8,128)(2,1)} %bitcast.104), calls=%async_computation.3 | async-start | bytes 262144 | tf_op jit(solution)/shard_map/all_to_all | solution.py:163
Sparse Core Ops, SparseCore 0:
  19.8 142.2 all-gather.3
  250.9 51.9 reduce-scatter.2
  305.3 30.9 all-gather.5
  344.7 217.6 reduce-scatter.4

commit v2 on v0

v2 whole, which is shorter than its diff:
```python
import functools
import jax
import jax.numpy as jnp
from jax import lax
from jax.experimental import pallas as pl
from jax.experimental.pallas import tpu as pltpu
from jax.sharding import PartitionSpec as P

BLOCK = 32
CAP = 4
TOK = 16
MESH = pl.DeviceIdType.MESH
BF, F32 = jnp.bfloat16, jnp.float32
PHASES = ((0, 0), (0, 1), (1, 0), (1, 1), (0, 2), (1, 2))


def loop(low, high, step):
    def one(i, c):
        step(i)
        return c

    lax.fori_loop(low, high, one, 0)


def layer(dims, rows, inv, scl, tok, meta, out, mixed,
          enc, got, s_in, s_flat, xcol, m_all, m_send, m_col, sbuf, slots, wgu, wdn,
          pa, pb, ra, rb, rc, hid, osend, orecv, pm, pr, fin,
          load_sem, e_send, e_recv, e_own, e_out, sc_sem, t_sem, m_sem, z_sem, zm_sem, x_sem,
          a_sem, b_sem, h_sem, i_sem, o_sem, p_sem, q_sem):
    nz, nx, ny, fs, unit = dims
    ne, nf = nz * nx, 2 * ny
    nb = fs // BLOCK
    gt, gs = nf * TOK, nf * CAP
    half = nz * gs // 2
    hidden = ne * unit
    ex, f = lax.axis_index("expert"), lax.axis_index("fsdp")
    z, x = ex // nx, lax.rem(ex, nx)
    y, core = f // 2, lax.rem(f, 2)
    mate = y * 2 + (1 - core)
    barrier = pltpu.get_barrier_semaphore()

    def to_expert(src, dst, send, recv, e):
        return pltpu.make_async_remote_copy(src_ref=src, dst_ref=dst, send_sem=send, recv_sem=recv,
                                            device_id={"expert": e}, device_id_type=MESH)

    def to_fsdp(src, dst, send, recv, g):
        return pltpu.make_async_remote_copy(src_ref=src, dst_ref=dst, send_sem=send, recv_sem=recv,
                                            device_id={"fsdp": g}, device_id_type=MESH)

    def local(src, dst, sem):
        return pltpu.make_async_copy(src, dst, sem)

    for ph, (k, p) in enumerate(PHASES):
        local(rows.at[:, k, p], enc.at[ph], load_sem.at[ph]).start()

    def greet_expert(j):
        pl.semaphore_signal(barrier, inc=1, device_id={"expert": lax.rem(ex + j, ne)}, device_id_type=MESH)

    def greet_fsdp(j):
        pl.semaphore_signal(barrier, inc=1, device_id={"fsdp": lax.rem(f + j, nf)}, device_id_type=MESH)

    loop(1, nf, greet_fsdp)
    loop(1, ne, greet_expert)
    pl.semaphore_wait(barrier, ne + nf - 2)

    def tok_send(j):
        g = lax.rem(f + j, nf)
        here = pl.ds(pl.multiple_of(f * TOK, TOK), TOK)
        to_fsdp(tok.at[:, pl.ds(pl.multiple_of(g * fs, fs), fs)], xcol.at[z, here], t_sem.at[0], t_sem.at[1], g).start()
        to_fsdp(meta, m_all.at[here], m_sem.at[0], m_sem.at[1], g).start()

    here = pl.ds(pl.multiple_of(f * TOK, TOK), TOK)
    loop(1, nf, tok_send)
    local(tok.at[:, pl.ds(pl.multiple_of(f * fs, fs), fs)], xcol.at[z, here], t_sem.at[2]).start()
    local(meta, m_all.at[here], m_sem.at[2]).start()

    def pick(ph):
        k, p = PHASES[ph]
        lane = lax.broadcasted_iota(jnp.int32, (128, fs), 0)
        feat = lax.broadcasted_iota(jnp.int32, (128, fs), 1)
        return (lane == (k * 3 + p) * nb + feat // BLOCK).astype(BF)

    per = min(8, ne)

    def encode(ph):
        local(rows.at[:, 0, 0], enc.at[ph], load_sem.at[ph]).wait()
        sel = pick(ph)

        def step(i):
            wide = jnp.dot(inv[pl.ds(pl.multiple_of(i * per * unit, per * unit), per * unit), :], sel, preferred_element_type=F32)
            for u in range(per):
                v = enc[ph, i * per + u].astype(F32) * wide[u * unit:(u + 1) * unit]
                v = jnp.minimum(jnp.maximum(v, -6.0), 6.0)
                a = jnp.abs(v)
                magic = jnp.where(a < 2.0, 6291456.0, jnp.where(a < 4.0, 12582912.0, 25165824.0))
                enc[ph, i * per + u] = ((v + magic) - magic).astype(BF)

        loop(0, ne // per, step)

    def zigzag(i):
        return lax.rem(ex + jnp.where(lax.rem(i, 2) == 1, (i + 1) // 2, ne - i // 2), ne)

    def elements_send(ph):
        def step(i):
            e = zigzag(i)
            to_expert(enc.at[ph, e], got.at[ph, ex], e_send.at[ph], e_recv.at[ph], e).start()

        loop(1, ne, step)
        local(enc.at[ph, ex], got.at[ph, ex], e_own.at[ph]).start()

    def scales_send(i):
        e = zigzag(i)
        to_expert(scl.at[e], s_in.at[ex], sc_sem.at[0], sc_sem.at[1], e).start()

    encode(0)

    many_f = pl.ds(0, (nf - 1) * TOK)
    local(xcol.at[z, many_f], xcol.at[z, many_f], t_sem.at[1]).wait()
    local(xcol.at[z, here], xcol.at[z, here], t_sem.at[2]).wait()
    local(m_all.at[many_f], m_all.at[many_f], m_sem.at[1]).wait()
    local(meta, m_all.at[here], m_sem.at[2]).wait()
    turned = jnp.transpose(m_all[...])
    m_send[...] = turned.reshape(128 // 16, 16, gt)[:nz]

    def z_send(j):
        to = lax.rem(z + j, nz)
        to_expert(xcol.at[z], xcol.at[z], z_sem.at[0], z_sem.at[1], to * nx + x).start()
        to_expert(m_send.at[to], m_col.at[z], zm_sem.at[0], zm_sem.at[1], to * nx + x).start()

    loop(1, nz, z_send)
    local(m_send.at[z], m_col.at[z], zm_sem.at[2]).start()
    loop(1, ne, scales_send)
    local(scl.at[ex], s_in.at[ex], sc_sem.at[2]).start()
    elements_send(0)
    encode(1)
    elements_send(1)

    many_z = pl.ds(0, nz - 1)
    local(xcol.at[many_z], xcol.at[many_z], z_sem.at[1]).wait()
    local(m_col.at[many_z], m_col.at[many_z], zm_sem.at[1]).wait()
    local(m_send.at[z], m_col.at[z], zm_sem.at[2]).wait()

    block4 = (lax.broadcasted_iota(jnp.int32, (2 * nx, gt), 1) // TOK * CAP).astype(F32)
    slot_of = lax.broadcasted_iota(jnp.int32, (gs, gt), 0).astype(F32)

    def targets(g):
        code = m_col[g, 0:2 * nx]
        return jnp.where(code > 0.5, block4 + code - 1.0, -1.0)

    def compact(g):
        tgt = targets(g)
        hot = jnp.concatenate([(slot_of == tgt[j:j + 1]).astype(F32) for j in range(2 * nx)], axis=0).astype(BF)
        taken = jnp.dot(hot, xcol[g], preferred_element_type=F32).astype(BF)
        for j in range(2 * nx):
            sbuf[j // 2, j % 2, pl.ds(pl.multiple_of(g * gs, gs), gs), :] = taken[j * gs:(j + 1) * gs]

    loop(0, nz, compact)

    for k in range(2):
        for j in range(1, nx):
            to = lax.rem(x + j, nx)
            to_expert(sbuf.at[to, k], slots.at[k, x], x_sem.at[0, k], x_sem.at[1, k], z * nx + to).start()
        local(sbuf.at[x, k], slots.at[k, x], x_sem.at[2, k]).start()

    for ph in range(2, 6):
        encode(ph)
        elements_send(ph)

    many_e = pl.ds(0, ne - 1)
    many_x = pl.ds(0, nx - 1)
    many_y = pl.ds(0, ny - 1)

    def elements_wait(ph):
        k, p = PHASES[ph]
        local(enc.at[ph, ex], got.at[ph, ex], e_own.at[ph]).wait()
        local(got.at[ph, many_e], got.at[ph, many_e], e_recv.at[ph]).wait()
        local(got.at[ph], out.at[k, p], e_out.at[ph]).start()

    def widen(ph, dst, base):
        sel = pick(ph)

        def step(i):
            at = pl.multiple_of(i * per * unit, per * unit)
            wide = jnp.dot(s_flat[pl.ds(at, per * unit), :], sel, preferred_element_type=F32)
            vals = [got[ph, i * per + u].astype(F32) * wide[u * unit:(u + 1) * unit] for u in range(per)]
            dst[pl.ds(base + at, per * unit), :] = jnp.concatenate(vals, axis=0).astype(BF)

        loop(0, ne // per, step)

    def gate_up(k, c, dst):
        lhs = slots[k, :, pl.ds(pl.multiple_of(c * half, half), half), :].reshape(nx * half, fs)
        cols = min(256, hidden)

        def step(n):
            at = pl.multiple_of(n * cols, cols)
            res = lax.dot_general(lhs, wgu[pl.ds(at, cols), :], (((1,), (1,)), ((), ())), preferred_element_type=F32)
            dst[k, :, :, pl.ds(at, cols)] = res.astype(BF).reshape(ny, half, cols)

        loop(0, 2 * hidden // cols, step)

    def first_sums(k):
        elements_wait(2 * k)
        widen(2 * k, wgu, 0)
        elements_wait(2 * k + 1)
        widen(2 * k + 1, wgu, hidden)
        local(slots.at[k, many_x], slots.at[k, many_x], x_sem.at[1, k]).wait()
        local(sbuf.at[x, k], slots.at[k, x], x_sem.at[2, k]).wait()
        gate_up(k, 1 - core, pa)
        to_fsdp(pa.at[k], ra.at[k], a_sem.at[0, k], a_sem.at[1, k], mate).start()
        gate_up(k, core, pb)
        local(pa.at[k], ra.at[k], a_sem.at[1, k]).wait()
        for j in range(ny):
            to = lax.rem(y + ny - 1 - j, ny)
            to = lax.rem(y + 1 + j, ny)
            rb[k, to] = (pb[k, to].astype(F32) + ra[k, to].astype(F32)).astype(BF)
            if j < ny - 1:
                to_fsdp(rb.at[k, to], rc.at[k, y], b_sem.at[0, k], b_sem.at[1, k], to * 2 + core).start()

    def activate(k):
        local(rc.at[k, many_y], rc.at[k, many_y], b_sem.at[1, k]).wait()
        total = rb[k, y].astype(F32)
        for j in range(1, ny):
            total = total + rc[k, lax.rem(y + j, ny)].astype(F32)
        gate, up = total[:, :hidden], total[:, hidden:]
        hid[k, core, y] = (gate / (1.0 + jnp.exp(-gate)) * up).astype(BF)
        for j in range(1, ny):
            to = lax.rem(y + j, ny)
            to_fsdp(hid.at[k, core, y], hid.at[k, core, y], h_sem.at[0, k], h_sem.at[1, k], to * 2 + core).start()

    def forward(k):
        local(hid.at[k, 0, many_y], hid.at[k, 0, many_y], h_sem.at[1, k]).wait()
        to_fsdp(hid.at[k, core], hid.at[k, core], i_sem.at[0, k], i_sem.at[1, k], mate).start()

    def down(k):
        local(hid.at[k, 0], hid.at[k, 0], i_sem.at[1, k]).wait()
        for j in range(nx):
            to = lax.rem(x + 1 + j, nx)
            lhs = jnp.concatenate([hid[k, 0, to], hid[k, 1, to]], axis=0)
            osend[k, to] = jnp.dot(lhs, wdn[...], preferred_element_type=F32).astype(BF)
            if j < nx - 1:
                to_expert(osend.at[k, to], orecv.at[k, x], o_sem.at[0, k], o_sem.at[1, k], z * nx + to).start()
            else:
                local(osend.at[k, to], orecv.at[k, to], o_sem.at[2, k]).start()

    local(scl.at[many_e], s_in.at[many_e], sc_sem.at[1]).wait()
    local(scl.at[ex], s_in.at[ex], sc_sem.at[2]).wait()

    def flatten(i):
        vals = [s_in[i * per + u].astype(F32) for u in range(per)]
        s_flat[pl.ds(pl.multiple_of(i * per * unit, per * unit), per * unit), :] = jnp.concatenate(vals, axis=0).astype(BF)

    loop(0, ne // per, flatten)

    first_sums(0)
    activate(0)
    forward(0)
    first_sums(1)
    elements_wait(4)
    widen(4, wdn, 0)
    down(0)
    activate(1)
    forward(1)
    elements_wait(5)
    widen(5, wdn, 0)
    down(1)

    for k in range(2):
        local(orecv.at[k, many_x], orecv.at[k, many_x], o_sem.at[1, k]).wait()
        local(osend.at[k, x], orecv.at[k, x], o_sem.at[2, k]).wait()

    def blend(j):
        g = lax.rem(z + j, nz)
        tgt = targets(g)
        share = m_col[g, 8:8 + 2 * nx]
        hot = jnp.concatenate([jnp.where(slot_of == tgt[i:i + 1], share[i:i + 1], 0.0) for i in range(2 * nx)], axis=0)
        hi = hot.astype(BF)
        lo = (hot - hi.astype(F32)).astype(BF)
        at = pl.ds(pl.multiple_of(g * gs, gs), gs)
        vals = jnp.concatenate([orecv[i % 2, i // 2, at, :] for i in range(2 * nx)], axis=0)
        both = (((0,), (0,)), ((), ()))
        part = lax.dot_general(hi, vals, both, preferred_element_type=F32)
        part = part + lax.dot_general(lo, vals, both, preferred_element_type=F32)
        pm[g] = part.astype(BF)

    def blend_send(j):
        blend(j)
        g = lax.rem(z + j, nz)
        to_expert(pm.at[g], pr.at[z], p_sem.at[0], p_sem.at[1], g * nx + x).start()

    loop(1, nz, blend_send)
    blend(0)
    local(pr.at[many_z], pr.at[many_z], p_sem.at[1]).wait()
    total = pm[z].astype(F32)
    for j in range(1, nz):
        total = total + pr[lax.rem(z + j, nz)].astype(F32)
    fin[...] = total.astype(BF)

    def fin_send(j):
        g = lax.rem(f + j, nf)
        to_fsdp(fin.at[pl.ds(pl.multiple_of(g * TOK, TOK), TOK)], mixed.at[:, pl.ds(pl.multiple_of(f * fs, fs), fs)],
                q_sem.at[0], q_sem.at[1], g).start()

    loop(1, nf, fin_send)
    mine = local(fin.at[here], mixed.at[:, pl.ds(pl.multiple_of(f * fs, fs), fs)], q_sem.at[2])
    mine.start()

    for ph, (k, p) in enumerate(PHASES):
        local(enc.at[ph, many_e], enc.at[ph, many_e], e_send.at[ph]).wait()
        local(got.at[ph], out.at[k, p], e_out.at[ph]).wait()
    local(scl.at[many_e], scl.at[many_e], sc_sem.at[0]).wait()
    local(xcol.at[z, many_f], xcol.at[z, many_f], t_sem.at[0]).wait()
    local(m_all.at[many_f], m_all.at[many_f], m_sem.at[0]).wait()
    local(xcol.at[many_z], xcol.at[many_z], z_sem.at[0]).wait()
    local(m_col.at[many_z], m_col.at[many_z], zm_sem.at[0]).wait()
    for k in range(2):
        local(slots.at[k, many_x], slots.at[k, many_x], x_sem.at[0, k]).wait()
        local(pa.at[k], pa.at[k], a_sem.at[0, k]).wait()
        local(rc.at[k, many_y], rc.at[k, many_y], b_sem.at[0, k]).wait()
        local(hid.at[k, 0, many_y], hid.at[k, 0, many_y], h_sem.at[0, k]).wait()
        local(hid.at[k, 0], hid.at[k, 0], i_sem.at[0, k]).wait()
        local(orecv.at[k, many_x], orecv.at[k, many_x], o_sem.at[0, k]).wait()
    local(pr.at[many_z], pr.at[many_z], p_sem.at[0]).wait()
    mine.wait()
    rest = mixed.at[:, pl.ds(0, (nf - 1) * fs)]
    local(rest, rest, q_sem.at[1]).wait()
    local(rest, rest, q_sem.at[0]).wait()


def run_layer(dims, rows, inv, scl, tok, meta):
    nz, nx, ny, fs, unit = dims
    ne, nf = nz * nx, 2 * ny
    gt, gs = nf * TOK, nf * CAP
    half, hidden = nz * gs // 2, ne * unit
    vm = pl.BlockSpec(memory_space=pltpu.VMEM)
    hbm = pl.BlockSpec(memory_space=pl.ANY)
    V = lambda *s: pltpu.VMEM(s, BF)
    dma = lambda *s: pltpu.SemaphoreType.DMA(s)
    return pl.pallas_call(
        functools.partial(layer, dims),
        out_shape=(jax.ShapeDtypeStruct((2, 3, ne, unit, fs), BF), jax.ShapeDtypeStruct((TOK, nf * fs), BF)),
        in_specs=[hbm, vm, vm, vm, vm],
        out_specs=(hbm, vm),
        scratch_shapes=[
            V(6, ne, unit, fs), V(6, ne, unit, fs), V(ne, unit, 128), V(hidden, 128),
            V(nz, gt, fs), pltpu.VMEM((gt, 128), F32), pltpu.VMEM((nz, 16, gt), F32), pltpu.VMEM((nz, 16, gt), F32),
            V(nx, 2, nz * gs, fs), V(2, nx, nz * gs, fs), V(2 * hidden, fs), V(hidden, fs),
            V(2, ny, half, 2 * hidden), V(2, ny, half, 2 * hidden), V(2, ny, half, 2 * hidden), V(2, ny, half, 2 * hidden), V(2, ny, half, 2 * hidden),
            V(2, 2, ny, half, hidden), V(2, nx, nz * gs, fs), V(2, nx, nz * gs, fs),
            V(nz, gt, fs), V(nz, gt, fs), V(gt, fs),
            dma(6), dma(6), dma(6), dma(6), dma(6), dma(3), dma(3), dma(3), dma(2), dma(3), dma(3, 2),
            dma(2, 2), dma(2, 2), dma(2, 2), dma(2, 2), dma(3, 2), dma(2), dma(3),
        ],
        compiler_params=pltpu.CompilerParams(collective_id=1, has_side_effects=True, vmem_limit_bytes=64000 * 1024),
        name="layer",
    )(rows, inv, scl, tok, meta)


def body(dims, tokens, learner_rows, exponents, expert_ids, route_probs):
    nz, nx, ny, fs, unit = dims
    ne = nz * nx
    nb = fs // BLOCK
    experts = 2 * ne
    exps = exponents.reshape(ne, 2, 3, unit, nb).transpose(0, 3, 1, 2, 4).reshape(ne, unit, 6 * nb).astype(F32)
    pad = ((0, 0), (0, 0), (0, 128 - 6 * nb))
    scl = jnp.pad(jnp.exp2(exps), pad).astype(BF)
    inv = jnp.pad(jnp.exp2(-exps), pad).astype(BF).reshape(ne * unit, 128)
    share = route_probs / jnp.sum(route_probs, axis=1, keepdims=True)
    hit = (expert_ids[:, :, None] == jnp.arange(experts, dtype=jnp.int32)).astype(F32)
    member = jnp.sum(hit, axis=1)
    weight = jnp.sum(hit * share[:, :, None], axis=1)
    order = jnp.arange(TOK)
    before = (order[None, :] < order[:, None]).astype(F32)
    code = member * (1.0 + jnp.dot(before, member))
    meta = jnp.zeros((TOK, 8, 16), F32)
    meta = meta.at[:, :nz, :2 * nx].set(code.reshape(TOK, nz, 2 * nx))
    meta = meta.at[:, :nz, 8:8 + 2 * nx].set(weight.reshape(TOK, nz, 2 * nx)).reshape(TOK, 128)
    el, mixed = run_layer(dims, learner_rows.reshape(ne, 2, 3, unit, fs), inv, scl, tokens, meta)
    return el.reshape(2, 3, ne * unit, fs), mixed


def make(mesh, dims):
    return jax.shard_map(
        functools.partial(body, dims),
        mesh=mesh,
        in_specs=(
            P(("fsdp", "expert"), None),
            P(None, None, "expert", "fsdp"),
            P(None, None, "expert", "fsdp"),
            P(("fsdp", "expert"), None),
            P(("fsdp", "expert"), None),
        ),
        out_specs=(P("expert", None, None, "fsdp"), P(("fsdp", "expert"), None)),
        check_vma=False,
    )


def solution(mesh):
    return make(mesh, (8, 4, 4, 512, 24))
```

time: 474 us -> 218 us (0.46)
  Pallas kernels: 0 us -> 202 us
  waiting for transfers between devices: 191 us -> 0 us
  local copies, waits for them, and re-layouts: 101 us -> 10.9 us
  blocking collectives: 87.3 us -> 0 us
  starting transfers between devices: 33.4 us -> 0 us
  other arithmetic: 29 us -> 2.76 us
  matrix products: 14.5 us -> 0.12 us
  between operations: 14.3 us -> 0.7 us
    pallas_call x0 -> x1, Pallas kernels: none -> 202 us  [run_layer(): pl.pallas_call(functools.partial(layer, dims), out_shape=(jax.ShapeDtypeS...]
    all_to_all x4 -> x0, waiting for transfers between devices: 116 us -> none  [the longest x1 89.8 us: body(): lax.all_to_all(element_view, 'expert', split_axis=0, concat_axis=3, tiled...]
    all_to_all x2 -> x0, blocking collectives: 87.3 us -> none  [the longest x1 58.1 us: body(): lax.all_to_all(lax.all_to_all(back_view, 'fsdp', split_axis=2, concat_axi...]
    reduce_scatter x1 -> x0, waiting for transfers between devices: 43.4 us -> none  [body(): lax.psum_scatter(partial_value.astype(jnp.bfloat16), 'fsdp', scatter_dime...]
    all_to_all x4 -> x0, starting transfers between devices: 33.3 us -> none  [the longest x1 10.3 us: body(): lax.all_to_all(scale_view, 'expert', split_axis=0, concat_axis=3, tiled=T...]
    all_gather x1 -> x0, waiting for transfers between devices: 31.1 us -> none  [body(): lax.all_gather(hidden, 'fsdp', axis=2, tiled=True)]
    unnamed x26 -> x6, local copies, waits for them, and re-layouts: 36.4 us -> 6.84 us
    convert_element_type x5 -> x0, other arithmetic: 25.6 us -> none  [the longest x1 23.1 us: to_grid(): return (jnp.sign(clipped) * level.astype(jnp.float32)).astype(jnp.bfloat16)]
  transfers between devices with their start and end apart: 6 -> 0, of which waited for: 5 -> 0; matrix products, arithmetic and copies ran while one was open for 17% -> 0% of each run, Pallas kernels for 0% -> 0%
where the time goes in v2:
time: 218 us; the launch traced here: 217 us
  Pallas kernels  202 us (93%)
  local copies, waits for them, and re-layouts  10.9 us (5%)
  other arithmetic  2.76 us (1%)
    pallas_call x1, Pallas kernels, run_layer(): pl.pallas_call(functools.partial(layer, dims), out_shape=(jax.ShapeDtypeS...  202 us
    unnamed x6, local copies, waits for them, and re-layouts  6.84 us

profile of v2, /device:TPU:1, one launch (start us, length us, event | category | flops | bytes accessed | tf_op | source)
XLA Modules:
  0.0 216.9 jit_solution(746668631387797798)
XLA Ops:
  0.6 0.7 reduce_sum.28
  1.3 0.7 broadcast_divide_fusion
  2.0 0.1 copy.29
  2.1 0.8 copy.27
  2.9 0.1 convert_reduce_fusion
  3.0 0.1 fusion
  3.1 0.1 copy.28
  3.2 0.1 copy.30
  3.3 0.7 copy.34.meta
  4.0 1.2 exponential_convert_fusion.1
  5.2 0.7 copy.24
  5.9 0.3 copy.26
  6.2 0.7 pad.15.scl
  6.9 0.7 copy.21
  7.7 0.3 copy.35
  7.9 0.7 pad.14.clone
  8.7 202.4 %layer.1 = (bf16[2,3,32,24,512]{4,3,2,1,0:T(8,128)(2,1)}, bf16[16,4096]{1,0:T(8,128)(2,1)}) custom-call(bf16[32,2,3,24,512]{4,3,2,1,0:T(8,128)(2,1)} %bitcast.18, bf16[768,128]{1,0:T(8,128)(2,1)} %bitcast.22, bf16[32,24,128]{2,1,0:T(8,128)(2,1)} %pad.15.scl, bf16[16,4096]{1,0:T(8,128)(2,1)} %tok.1, f32[16,128]{1,0:T(8,128)} %copy.34.meta), custom_call_target="tpu_custom_call" | custom-call | tf_op jit(solution)/shard_map/layer/pallas_call | solution.py:338
  211.1 0.0 copy-start
  211.1 5.1 %copy.39 = bf16[2,3,768,512]{3,2,1,0:T(8,128)(2,1)} copy(bf16[2,3,768,512]{3,2,1,0:T(8,128)(2,1)} %bitcast.19) | data formatting | bytes 9437184
  216.2 0.0 copy-done
  216.2 0.7 copy.40
  (1 shorter events, 0.0 us)
Async XLA Ops:
  211.1 5.2 %copy-start = (bf16[16,4096]{1,0:T(8,128)(2,1)S(1)}, bf16[16,4096]{1,0:T(8,128)(2,1)}, u32[]{:S(2)}) copy-start(bf16[16,4096]{1,0:T(8,128)(2,1)} %get-tuple-element.37) | copy-start | bytes 393220

commit v3 on v2

v3 whole, which is shorter than its diff:
```python
import functools
import jax
import jax.numpy as jnp
from jax import lax
from jax.experimental import pallas as pl
from jax.experimental.pallas import tpu as pltpu
from jax.sharding import PartitionSpec as P

BLOCK = 32
CAP = 4
NEAR = 20
VMEM_LIMIT = 64000 * 1024
TOK = 16
MESH = pl.DeviceIdType.MESH
BF, F32 = jnp.bfloat16, jnp.float32
PHASES = ((0, 0), (0, 1), (1, 0), (1, 1), (0, 2), (1, 2))
PARTS = ((0, 0, 2), (1, 0, 2), (2, 0, 2), (3, 0, 2), (4, 0, 1), (5, 0, 1), (4, 1, 1), (5, 1, 1))


def loop(low, high, step):
    def one(i, c):
        step(i)
        return c

    lax.fori_loop(low, high, one, 0)


def layer(dims, rows, exps, tok, packed, out, mixed,
          enc, got, inv_t, scl_t, s_out, s_in, meta, xcol, m_all, m_send, m_col, sbuf, slots, wgu, wdn,
          pa, pb, ra, rb, rc, hid, osend, orecv, pm, up_sum, dn_sum, fin,
          load_sem, e_send, e_recv, e_own, e_out, sc_sem, t_sem, m_sem, zu_sem, zd_sem, zm_sem, x_sem,
          x_own, a_sem, b_sem, h_sem, i_sem, o_sem, o_own, pu_sem, pd_sem, q_sem):
    nz, nx, ny, fs, unit = dims
    ne, nf = nz * nx, 2 * ny
    nb = fs // BLOCK
    gt, gs = nf * TOK, nf * CAP
    half = nz * gs // 2
    hidden = ne * unit
    wide_half = fs // 2
    chunk = half // 2
    experts, span = 2 * ne, unit * nb
    ups, downs = nz // 2, (nz - 1) // 2
    ex, f = lax.axis_index("expert"), lax.axis_index("fsdp")
    z, x = ex // nx, lax.rem(ex, nx)
    y, core = f // 2, lax.rem(f, 2)
    mate = y * 2 + (1 - core)
    barrier = pltpu.get_barrier_semaphore()

    def to_expert(src, dst, send, recv, e):
        return pltpu.make_async_remote_copy(src_ref=src, dst_ref=dst, send_sem=send, recv_sem=recv,
                                            device_id={"expert": e}, device_id_type=MESH)

    def to_fsdp(src, dst, send, recv, g):
        return pltpu.make_async_remote_copy(src_ref=src, dst_ref=dst, send_sem=send, recv_sem=recv,
                                            device_id={"fsdp": g}, device_id_type=MESH)

    def local(src, dst, sem):
        return pltpu.make_async_copy(src, dst, sem)

    def at_z(d):
        return lax.rem(z + d + nz, nz)

    for ph, (k, p) in enumerate(PHASES):
        local(rows.at[:, k, p], enc.at[ph], load_sem.at[ph]).start()

    def greet_expert(j):
        pl.semaphore_signal(barrier, inc=1, device_id={"expert": lax.rem(ex + j, ne)}, device_id_type=MESH)

    def greet_fsdp(j):
        pl.semaphore_signal(barrier, inc=1, device_id={"fsdp": lax.rem(f + j, nf)}, device_id_type=MESH)

    loop(1, nf, greet_fsdp)
    loop(1, ne, greet_expert)
    ids, probs = packed[0:8], packed[8:16]
    share = probs / jnp.sum(probs, axis=0, keepdims=True)
    expert_of = lax.broadcasted_iota(jnp.int32, (experts, 128), 0).astype(F32)
    member = jnp.zeros((experts, 128), F32)
    weight = jnp.zeros((experts, 128), F32)
    for i in range(8):
        hit = expert_of == ids[i:i + 1]
        member = member + hit.astype(F32)
        weight = weight + jnp.where(hit, share[i:i + 1], 0.0)
    before = lax.broadcasted_iota(jnp.int32, (128, 128), 0) < lax.broadcasted_iota(jnp.int32, (128, 128), 1)
    code = member * (1.0 + jnp.dot(member.astype(BF), before.astype(BF), preferred_element_type=F32))
    row_list = []
    for i in range(8):
        own = slice(i * 2 * nx, (i + 1) * 2 * nx)
        for table in (code, weight):
            if i < nz:
                row_list.append(table[own])
                if 2 * nx < 8:
                    row_list.append(jnp.zeros((8 - 2 * nx, 128), F32))
            else:
                row_list.append(jnp.zeros((8, 128), F32))
    meta[...] = jnp.transpose(jnp.concatenate(row_list, axis=0))[:TOK]

    for p in range(3):
        flat = exps[p].reshape(span, experts).astype(F32)
        if experts < 128:
            flat = jnp.concatenate([flat, jnp.zeros((span, 128 - experts), F32)], axis=1)
        turned = jnp.transpose(flat)[:experts]
        inv_t[p] = jnp.exp2(-turned).astype(BF).astype(F32)
        scl_t[p] = jnp.exp2(turned).astype(BF).astype(F32)

    def gather_scales(o):
        lines = [scl_t[p, pl.ds(o * 2 + k, 1), :] for k in range(2) for p in range(3)]
        s_out[o] = jnp.concatenate(lines + [jnp.zeros((2, span), F32)], axis=0).astype(BF)

    loop(0, ne, gather_scales)

    spread_row = lax.broadcasted_iota(jnp.int32, (unit, span), 0)
    spread_lane = lax.broadcasted_iota(jnp.int32, (unit, span), 1)
    diagonal = spread_lane // nb == spread_row

    def pick(at=0, width=None):
        width = width or fs
        lane = lax.broadcasted_iota(jnp.int32, (span, width), 0)
        feat = lax.broadcasted_iota(jnp.int32, (span, width), 1) + at
        return (lax.rem(lane, nb) == feat // BLOCK).astype(BF)

    per = min(8, ne)

    def encode(ph):
        local(rows.at[:, 0, 0], enc.at[ph], load_sem.at[ph]).wait()
        k, p = PHASES[ph]
        sel = pick()

        def step(i):
            lines = [jnp.where(diagonal, inv_t[p, pl.ds((i * per + u) * 2 + k, 1), :], 0.0) for u in range(per)]
            wide = jnp.dot(jnp.concatenate(lines, axis=0).astype(BF), sel, preferred_element_type=F32)
            for u in range(per):
                v = enc[ph, i * per + u].astype(F32) * wide[u * unit:(u + 1) * unit]
                v = jnp.minimum(jnp.maximum(v, -6.0), 6.0)
                a = jnp.abs(v)
                magic = jnp.where(a < 2.0, 6291456.0, jnp.where(a < 4.0, 12582912.0, 25165824.0))
                enc[ph, i * per + u] = ((v + magic) - magic).astype(BF)

        loop(0, ne // per, step)

    def zigzag(i):
        return lax.rem(ex + jnp.where(lax.rem(i, 2) == 1, (i + 1) // 2, ne - i // 2), ne)

    def part(n, ref, who):
        ph, lo, width = PARTS[n]
        return ref.at[ph, who] if width == 2 else ref.at[ph, who, :, pl.ds(lo * wide_half, wide_half)]

    def elements_some(n, low, high):
        def step(i):
            e = zigzag(i)
            to_expert(part(n, enc, e), part(n, got, ex), e_send.at[n], e_recv.at[n], e).start()

        loop(low, high, step)

    def elements_send(n):
        elements_some(n, 1, ne)
        local(part(n, enc, ex), part(n, got, ex), e_own.at[n]).start()

    def scales_send(i):
        e = zigzag(i)
        to_expert(s_out.at[e], s_in.at[ex], sc_sem.at[0], sc_sem.at[1], e).start()

    encode(0)
    encode(1)
    pl.semaphore_wait(barrier, ne + nf - 2)

    def tok_send(j):
        g = lax.rem(f + j, nf)
        here = pl.ds(pl.multiple_of(f * TOK, TOK), TOK)
        to_fsdp(tok.at[:, pl.ds(pl.multiple_of(g * fs, fs), fs)], xcol.at[z, here], t_sem.at[0], t_sem.at[1], g).start()
        to_fsdp(meta, m_all.at[here], m_sem.at[0], m_sem.at[1], g).start()

    here = pl.ds(pl.multiple_of(f * TOK, TOK), TOK)
    loop(1, nf, tok_send)
    local(tok.at[:, pl.ds(pl.multiple_of(f * fs, fs), fs)], xcol.at[z, here], t_sem.at[2]).start()
    local(meta, m_all.at[here], m_sem.at[2]).start()
    near = NEAR if ne > 16 else 2
    elements_some(0, 1, near)
    local(part(0, enc, ex), part(0, got, ex), e_own.at[0]).start()

    many_f = pl.ds(0, (nf - 1) * TOK)
    local(xcol.at[z, many_f], xcol.at[z, many_f], t_sem.at[1]).wait()
    local(xcol.at[z, here], xcol.at[z, here], t_sem.at[2]).wait()

    def cut(h, g):
        return xcol.at[g, :, pl.ds(h * wide_half, wide_half)]

    def push_up(h, step):
        g = at_z(1 - step)
        to_expert(cut(h, g), cut(h, g), zu_sem.at[0, h, step - 1], zu_sem.at[1, h, step - 1], at_z(1) * nx + x).start()

    def push_down(h, step):
        g = at_z(step - 1)
        to_expert(cut(h, g), cut(h, g), zd_sem.at[0, h, step - 1], zd_sem.at[1, h, step - 1], at_z(-1) * nx + x).start()

    for h in range(2):
        push_up(h, 1)
        if downs:
            push_down(h, 1)
    local(m_all.at[many_f], m_all.at[many_f], m_sem.at[1]).wait()
    local(meta, m_all.at[here], m_sem.at[2]).wait()
    turned = jnp.transpose(m_all[...])
    m_send[...] = turned.reshape(128 // 16, 16, gt)[:nz]

    def table_send(j):
        to = lax.rem(z + j, nz)
        to_expert(m_send.at[to], m_col.at[z], zm_sem.at[0], zm_sem.at[1], to * nx + x).start()

    loop(1, nz, table_send)
    local(m_send.at[z], m_col.at[z], zm_sem.at[2]).start()
    many_z = pl.ds(0, nz - 1)

    block4 = (lax.broadcasted_iota(jnp.int32, (2 * nx, gt), 1) // TOK * CAP).astype(F32)
    slot_of = lax.broadcasted_iota(jnp.int32, (gs, gt), 0).astype(F32)

    def targets(g):
        code = m_col[g, 0:2 * nx]
        return jnp.where(code > 0.5, block4 + code - 1.0, -1.0)

    def compact(g):
        tgt = targets(g)
        hot = jnp.concatenate([(slot_of == tgt[j:j + 1]).astype(F32) for j in range(2 * nx)], axis=0).astype(BF)
        taken = jnp.dot(hot, xcol[g], preferred_element_type=F32).astype(BF)
        at = pl.ds(pl.multiple_of(g * gs, gs), gs)
        for j in range(2 * nx):
            sbuf[j // 2, j % 2, at, :] = taken[j * gs:(j + 1) * gs]
        for j in range(1, nx):
            to = lax.rem(x + j, nx)
            to_expert(sbuf.at[to, 0, at], slots.at[0, x, at], x_sem.at[0, 0], x_sem.at[1, 0], z * nx + to).start()

    local(m_send.at[z], m_col.at[z], zm_sem.at[2]).wait()
    compact(z)
    for step in range(1, ups + 1):
        for h in range(2):
            local(cut(0, 0), cut(0, 0), zu_sem.at[1, h, step - 1]).wait()
            if step < ups:
                push_up(h, step + 1)
            if step <= downs:
                local(cut(0, 0), cut(0, 0), zd_sem.at[1, h, step - 1]).wait()
                if step < downs:
                    push_down(h, step + 1)
        if step == 1:
            local(m_col.at[many_z], m_col.at[many_z], zm_sem.at[1]).wait()
        if step == max(ups - 1, 1):
            loop(1, ne, scales_send)
            local(s_out.at[ex], s_in.at[ex], sc_sem.at[2]).start()
            elements_some(0, near, ne)
        compact(at_z(-step))
        if step <= downs:
            compact(at_z(step))

    local(sbuf.at[x, 0], slots.at[0, x], x_own.at[0]).start()
    elements_send(1)
    encode(2)
    elements_send(2)
    for j in range(1, nx):
        to = lax.rem(x + j, nx)
        to_expert(sbuf.at[to, 1], slots.at[1, x], x_sem.at[0, 1], x_sem.at[1, 1], z * nx + to).start()
    local(sbuf.at[x, 1], slots.at[1, x], x_own.at[1]).start()
    encode(3)
    elements_send(3)
    encode(4)
    elements_send(4)
    encode(5)
    for n in range(5, 8):
        elements_send(n)

    many_e = pl.ds(0, ne - 1)
    many_x = pl.ds(0, nx - 1)
    many_y = pl.ds(0, ny - 1)

    def elements_wait(n):
        ph, lo, width = PARTS[n]
        k, p = PHASES[ph]
        own, all_in = part(n, got, ex), part(n, got, many_e)
        local(own, own, e_own.at[n]).wait()
        local(all_in, all_in, e_recv.at[n]).wait()
        if lo + width == 2:
            local(got.at[ph], out.at[k, p], e_out.at[ph]).start()

    def widen(n, dst, base):
        ph, lo, width = PARTS[n]
        k, p = PHASES[ph]
        cols = width * wide_half
        sel = pick(lo * wide_half, cols)

        def step(i):
            at = pl.multiple_of(i * per * unit, per * unit)
            lines = [jnp.where(diagonal, s_in[i * per + u].astype(F32)[k * 3 + p:k * 3 + p + 1], 0.0) for u in range(per)]
            wide = jnp.dot(jnp.concatenate(lines, axis=0).astype(BF), sel, preferred_element_type=F32)
            vals = [got[ph, i * per + u, :, pl.ds(lo * wide_half, cols)].astype(F32) * wide[u * unit:(u + 1) * unit] for u in range(per)]
            dst[pl.ds(base + at, per * unit), :] = jnp.concatenate(vals, axis=0).astype(BF)

        loop(0, ne // per, step)

    def gate_up(k, c, dst, which):
        lhs = slots[k, :, pl.ds(pl.multiple_of(which * half + c * chunk, chunk), chunk), :].reshape(nx * chunk, fs)
        cols = min(256, hidden)

        def step(n):
            at = pl.multiple_of(n * cols, cols)
            res = lax.dot_general(lhs, wgu[pl.ds(at, cols), :], (((1,), (1,)), ((), ())), preferred_element_type=F32)
            dst[k, c, :, :, pl.ds(at, cols)] = res.astype(BF).reshape(ny, chunk, cols)

        loop(0, 2 * hidden // cols, step)

    def first_sums(k):
        elements_wait(2 * k)
        widen(2 * k, wgu, 0)
        elements_wait(2 * k + 1)
        widen(2 * k + 1, wgu, hidden)
        local(slots.at[k, many_x], slots.at[k, many_x], x_sem.at[1, k]).wait()
        local(sbuf.at[x, k], slots.at[k, x], x_own.at[k]).wait()
        for c in range(2):
            gate_up(k, c, pa, 1 - core)
            to_fsdp(pa.at[k, c], ra.at[k, c], a_sem.at[0, k, c], a_sem.at[1, k, c], mate).start()
            gate_up(k, c, pb, core)
        for c in range(2):
            local(pa.at[k, c], ra.at[k, c], a_sem.at[1, k, c]).wait()
            for j in range(ny):
                to = lax.rem(y + 1 + j, ny)
                rb[k, c, to] = (pb[k, c, to].astype(F32) + ra[k, c, to].astype(F32)).astype(BF)
                if j < ny - 1:
                    to_fsdp(rb.at[k, c, to], rc.at[k, c, y], b_sem.at[0, k, c], b_sem.at[1, k, c], to * 2 + core).start()

    def activate(k, c):
        local(rc.at[k, c, many_y], rc.at[k, c, many_y], b_sem.at[1, k, c]).wait()
        total = rb[k, c, y].astype(F32)
        for j in range(1, ny):
            total = total + rc[k, c, lax.rem(y + j, ny)].astype(F32)
        gate, up = total[:, :hidden], total[:, hidden:]
        hid[k, c, core, y] = (gate / (1.0 + jnp.exp(-gate)) * up).astype(BF)
        for j in range(1, ny):
            to = lax.rem(y + j, ny)
            to_fsdp(hid.at[k, c, core, y], hid.at[k, c, core, y], h_sem.at[0, k, c], h_sem.at[1, k, c], to * 2 + core).start()

    def forward(k, c):
        local(hid.at[k, c, 0, many_y], hid.at[k, c, 0, many_y], h_sem.at[1, k, c]).wait()
        to_fsdp(hid.at[k, c, core], hid.at[k, c, core], i_sem.at[0, k, c], i_sem.at[1, k, c], mate).start()

    def hidden_wait(k, c):
        local(hid.at[k, c, 0], hid.at[k, c, 0], i_sem.at[1, k, c]).wait()

    def down(k, h, c):
        for j in range(nx):
            to = lax.rem(x + 1 + j, nx)
            lhs = jnp.concatenate([hid[k, c, 0, to], hid[k, c, 1, to]], axis=0)
            osend[h, k, c, to] = jnp.dot(lhs, wdn[h], preferred_element_type=F32).astype(BF)
            if j < nx - 1:
                to_expert(osend.at[h, k, c, to], orecv.at[h, k, c, x], o_sem.at[0, h, k, c], o_sem.at[1, h, k, c], z * nx + to).start()
            else:
                local(osend.at[h, k, c, to], orecv.at[h, k, c, to], o_own.at[h, k, c]).start()

    def outputs_wait(h):
        for k in range(2):
            for c in range(2):
                local(orecv.at[h, k, c, many_x], orecv.at[h, k, c, many_x], o_sem.at[1, h, k, c]).wait()
                local(osend.at[h, k, c, x], orecv.at[h, k, c, x], o_own.at[h, k, c]).wait()

    def blend(h, g):
        tgt = targets(g)
        share = m_col[g, 8:8 + 2 * nx]
        hot = jnp.concatenate([jnp.where(slot_of == tgt[i:i + 1], share[i:i + 1], 0.0) for i in range(2 * nx)], axis=0)
        hi = hot.astype(BF)
        lo = (hot - hi.astype(F32)).astype(BF)
        which, inside = g // (nz // 2), lax.rem(g, nz // 2) * gs
        c, spot = inside // chunk, lax.rem(inside, chunk)
        at = pl.ds(pl.multiple_of(which * chunk + spot, gs), gs)
        vals = jnp.concatenate([orecv[h, i % 2, c, i // 2, at, :] for i in range(2 * nx)], axis=0)
        both = (((0,), (0,)), ((), ()))
        res = lax.dot_general(hi, vals, both, preferred_element_type=F32)
        return res + lax.dot_general(lo, vals, both, preferred_element_type=F32)

    def sum_up(h, step):
        g = at_z(ups + 1 - step)
        val = blend(h, g)
        if step > 1:
            local(up_sum.at[h, 0], up_sum.at[h, 0], pu_sem.at[1, h, step - 2]).wait()
            val = val + up_sum[h, step - 2].astype(F32)
        pm[h, 0, step - 1] = val.astype(BF)
        to_expert(pm.at[h, 0, step - 1], up_sum.at[h, step - 1], pu_sem.at[0, h, step - 1], pu_sem.at[1, h, step - 1], at_z(1) * nx + x).start()

    def sum_down(h, step):
        g = at_z(step - downs - 1)
        val = blend(h, g)
        if step > 1:
            local(dn_sum.at[h, 0], dn_sum.at[h, 0], pd_sem.at[1, h, step - 2]).wait()
            val = val + dn_sum[h, step - 2].astype(F32)
        pm[h, 1, step - 1] = val.astype(BF)
        to_expert(pm.at[h, 1, step - 1], dn_sum.at[h, step - 1], pd_sem.at[0, h, step - 1], pd_sem.at[1, h, step - 1], at_z(-1) * nx + x).start()

    def ring(h, step):
        sum_up(h, step)
        if step <= downs:
            sum_down(h, step)

    def finish(h):
        val = blend(h, z)
        local(up_sum.at[h, 0], up_sum.at[h, 0], pu_sem.at[1, h, ups - 1]).wait()
        val = val + up_sum[h, ups - 1].astype(F32)
        if downs:
            local(dn_sum.at[h, 0], dn_sum.at[h, 0], pd_sem.at[1, h, downs - 1]).wait()
            val = val + dn_sum[h, downs - 1].astype(F32)
        fin[h] = val.astype(BF)
        cols = pl.ds(pl.multiple_of(f * fs + h * wide_half, wide_half), wide_half)

        def fin_send(j):
            g = lax.rem(f + j, nf)
            to_fsdp(fin.at[h, pl.ds(pl.multiple_of(g * TOK, TOK), TOK)], mixed.at[:, cols], q_sem.at[0, h], q_sem.at[1, h], g).start()

        loop(1, nf, fin_send)
        local(fin.at[h, here], mixed.at[:, cols], q_sem.at[2, h]).start()

    local(s_in.at[many_e], s_in.at[many_e], sc_sem.at[1]).wait()
    local(s_out.at[ex], s_in.at[ex], sc_sem.at[2]).wait()

    first_sums(0)
    for c in range(2):
        activate(0, c)
    for c in range(2):
        forward(0, c)
    first_sums(1)
    elements_wait(4)
    widen(4, wdn.at[0], 0)
    for c in range(2):
        hidden_wait(0, c)
        down(0, 0, c)
    activate(1, 0)
    elements_wait(6)
    widen(6, wdn.at[1], 0)
    for c in range(2):
        down(0, 1, c)
    activate(1, 1)
    forward(1, 0)
    elements_wait(5)
    widen(5, wdn.at[0], 0)
    hidden_wait(1, 0)
    down(1, 0, 0)
    elements_wait(7)
    widen(7, wdn.at[1], 0)
    down(1, 1, 0)
    forward(1, 1)
    hidden_wait(1, 1)
    down(1, 0, 1)
    down(1, 1, 1)
    outputs_wait(0)
    ring(0, 1)
    outputs_wait(1)
    for step in range(1, ups + 1):
        ring(1, step)
        if step < ups:
            ring(0, step + 1)
    finish(0)
    finish(1)

    for n in range(8):
        out_n = part(n, enc, many_e)
        local(out_n, out_n, e_send.at[n]).wait()
    for ph, (k, p) in enumerate(PHASES):
        local(got.at[ph], out.at[k, p], e_out.at[ph]).wait()
    local(s_in.at[many_e], s_in.at[many_e], sc_sem.at[0]).wait()
    local(xcol.at[z, many_f], xcol.at[z, many_f], t_sem.at[0]).wait()
    local(m_all.at[many_f], m_all.at[many_f], m_sem.at[0]).wait()
    for h in range(2):
        for step in range(ups):
            local(cut(0, 0), cut(0, 0), zu_sem.at[0, h, step]).wait()
        for step in range(downs):
            local(cut(0, 0), cut(0, 0), zd_sem.at[0, h, step]).wait()
    local(m_col.at[many_z], m_col.at[many_z], zm_sem.at[0]).wait()
    for k in range(2):
        local(slots.at[k, many_x], slots.at[k, many_x], x_sem.at[0, k]).wait()
        for c in range(2):
            local(pa.at[k, c], pa.at[k, c], a_sem.at[0, k, c]).wait()
            local(rc.at[k, c, many_y], rc.at[k, c, many_y], b_sem.at[0, k, c]).wait()
            local(hid.at[k, c, 0, many_y], hid.at[k, c, 0, many_y], h_sem.at[0, k, c]).wait()
            local(hid.at[k, c, 0], hid.at[k, c, 0], i_sem.at[0, k, c]).wait()
    for h in range(2):
        for k in range(2):
            for c in range(2):
                local(orecv.at[h, k, c, many_x], orecv.at[h, k, c, many_x], o_sem.at[0, h, k, c]).wait()
        for step in range(ups):
            local(up_sum.at[h, 0], up_sum.at[h, 0], pu_sem.at[0, h, step]).wait()
        for step in range(downs):
            local(dn_sum.at[h, 0], dn_sum.at[h, 0], pd_sem.at[0, h, step]).wait()
        mine = fin.at[h, here]
        local(mine, mine, q_sem.at[2, h]).wait()
        rest = fin.at[h, many_f]
        local(rest, rest, q_sem.at[1, h]).wait()
        local(rest, rest, q_sem.at[0, h]).wait()


def run_layer(dims, rows, exps, tok, packed):
    nz, nx, ny, fs, unit = dims
    ne, nf = nz * nx, 2 * ny
    gt, gs = nf * TOK, nf * CAP
    half, hidden, ups = nz * gs // 2, ne * unit, nz // 2
    chunk, hw, span = half // 2, fs // 2, unit * (fs // BLOCK)
    vm = pl.BlockSpec(memory_space=pltpu.VMEM)
    hbm = pl.BlockSpec(memory_space=pl.ANY)
    V = lambda *s: pltpu.VMEM(s, BF)
    W = lambda *s: pltpu.VMEM(s, F32)
    dma = lambda *s: pltpu.SemaphoreType.DMA(s)
    sums = [V(2, 2, ny, chunk, 2 * hidden)] * 5
    return pl.pallas_call(
        functools.partial(layer, dims),
        out_shape=(jax.ShapeDtypeStruct((2, 3, ne, unit, fs), BF), jax.ShapeDtypeStruct((TOK, nf * fs), BF)),
        in_specs=[hbm, vm, vm, vm],
        out_specs=(hbm, vm),
        scratch_shapes=[
            V(6, ne, unit, fs), V(6, ne, unit, fs), W(3, 2 * ne, span), W(3, 2 * ne, span), V(ne, 8, span), V(ne, 8, span),
            W(TOK, 128), V(nz, gt, fs), W(gt, 128), W(nz, 16, gt), W(nz, 16, gt),
            V(nx, 2, nz * gs, fs), V(2, nx, nz * gs, fs), V(2 * hidden, fs), V(2, hidden, hw),
            *sums,
            V(2, 2, 2, ny, chunk, hidden), V(2, 2, 2, nx, 2 * chunk, hw), V(2, 2, 2, nx, 2 * chunk, hw),
            V(2, 2, ups, gt, hw), V(2, ups, gt, hw), V(2, ups, gt, hw), V(2, gt, hw),
            dma(6), dma(8), dma(8), dma(8), dma(6), dma(3), dma(3), dma(3), dma(2, 2, ups), dma(2, 2, ups), dma(3), dma(2, 2), dma(2),
            dma(2, 2, 2), dma(2, 2, 2), dma(2, 2, 2), dma(2, 2, 2), dma(2, 2, 2, 2), dma(2, 2, 2), dma(2, 2, ups), dma(2, 2, ups), dma(3, 2),
        ],
        compiler_params=pltpu.CompilerParams(collective_id=1, has_side_effects=True, vmem_limit_bytes=VMEM_LIMIT),
        name="layer",
    )(rows, exps, tok, packed)


def body(dims, tokens, learner_rows, exponents, expert_ids, route_probs):
    nz, nx, ny, fs, unit = dims
    ne = nz * nx
    top = expert_ids.shape[1]
    ids = jnp.pad(expert_ids.T.astype(F32), ((0, 8 - top), (0, 128 - TOK)), constant_values=-1.0)
    probs = jnp.pad(jnp.pad(route_probs.T, ((0, 8 - top), (0, 0))), ((0, 0), (0, 128 - TOK)), constant_values=1.0)
    packed = jnp.concatenate([ids, probs], axis=0)
    el, mixed = run_layer(dims, learner_rows.reshape(ne, 2, 3, unit, fs), exponents.transpose(1, 2, 3, 0), tokens, packed)
    return el.reshape(2, 3, ne * unit, fs), mixed


def make(mesh, dims):
    return jax.shard_map(
        functools.partial(body, dims),
        mesh=mesh,
        in_specs=(
            P(("fsdp", "expert"), None),
            P(None, None, "expert", "fsdp"),
            P(None, None, "expert", "fsdp"),
            P(("fsdp", "expert"), None),
            P(("fsdp", "expert"), None),
        ),
        out_specs=(P("expert", None, None, "fsdp"), P(("fsdp", "expert"), None)),
        check_vma=False,
    )


def solution(mesh):
    return make(mesh, (8, 4, 4, 512, 24))
```

time: 218 us -> 185 us (0.85)
  Pallas kernels: 202 us -> 176 us
  local copies, waits for them, and re-layouts: 10.9 us -> 5.81 us
    pallas_call x1, Pallas kernels: 202 us -> 176 us  [run_layer(): pl.pallas_call(functools.partial(layer, dims), out_shape=(jax.ShapeDtypeS...]
    unnamed x6 -> x4, local copies, waits for them, and re-layouts: 6.84 us -> 5.81 us
where the time goes in v3:
time: 185 us; the launch traced here: 184 us
  Pallas kernels  176 us (95%)
  local copies, waits for them, and re-layouts  5.81 us (3%)
  other arithmetic  1.98 us (1%)
    pallas_call x1, Pallas kernels, run_layer(): pl.pallas_call(functools.partial(layer, dims), out_shape=(jax.ShapeDtypeS...  176 us
    unnamed x4, local copies, waits for them, and re-layouts  5.81 us

profile of v3, /device:TPU:1, one launch (start us, length us, event | category | flops | bytes accessed | tf_op | source)
XLA Modules:
  0.0 184.5 jit_solution(5730311380273078891)
XLA Ops:
  0.6 0.7 convert_bitcast_fusion
  1.3 1.3 select_maximum_fusion.packed
  2.6 176.1 %layer.1 = (bf16[2,3,32,24,512]{4,3,2,1,0:T(8,128)(2,1)}, bf16[16,4096]{1,0:T(8,128)(2,1)}) custom-call(bf16[32,2,3,24,512]{4,3,2,1,0:T(8,128)(2,1)} %bitcast.7, s32[3,24,16,64]{3,2,1,0:T(8,128)} %bitcast.8, bf16[16,4096]{1,0:T(8,128)(2,1)} %tok.1, f32[16,128]{1,0:T(8,128)} %select_maximum_fusion.packed), custom_call_target="tpu_custom_call" | custom-call | tf_op jit(solution)/shard_map/layer/pallas_call | solution.py:503
  178.7 0.0 copy-start
  178.7 5.1 %copy.9 = bf16[2,3,768,512]{3,2,1,0:T(8,128)(2,1)} copy(bf16[2,3,768,512]{3,2,1,0:T(8,128)(2,1)} %bitcast.6) | data formatting | bytes 9437184
  183.8 0.0 copy-done
  183.8 0.7 copy.10
Async XLA Ops:
  178.7 5.2 %copy-start = (bf16[16,4096]{1,0:T(8,128)(2,1)S(1)}, bf16[16,4096]{1,0:T(8,128)(2,1)}, u32[]{:S(2)}) copy-start(bf16[16,4096]{1,0:T(8,128)(2,1)} %get-tuple-element.9) | copy-start | bytes 393220

commit v4 on v3

--- a/solution.py
+++ b/solution.py
@@ -9,12 +9,14 @@
 BLOCK = 32
 CAP = 4
 NEAR = 20
-VMEM_LIMIT = 64000 * 1024
+SLICES = ((0, 20, 26), (0, 26, 32), (1, 1, 16), (1, 16, 24), (1, 24, 32))
+VMEM_LIMIT = 47 * 1024 * 1024
 TOK = 16
 MESH = pl.DeviceIdType.MESH
 BF, F32 = jnp.bfloat16, jnp.float32
 PHASES = ((0, 0), (0, 1), (1, 0), (1, 1), (0, 2), (1, 2))
-PARTS = ((0, 0, 2), (1, 0, 2), (2, 0, 2), (3, 0, 2), (4, 0, 1), (5, 0, 1), (4, 1, 1), (5, 1, 1))
+PIECES = 2
+PARTS = tuple((ph, 0, PIECES) for ph in range(4)) + tuple((ph, h, 1) for ph in (4, 5) for h in range(PIECES))
 
 
 def loop(low, high, step):
@@ -25,10 +27,10 @@
     lax.fori_loop(low, high, one, 0)
 
 
-def layer(dims, rows, exps, tok, packed, out, mixed,
-          enc, got, inv_t, scl_t, s_out, s_in, meta, xcol, m_all, m_send, m_col, sbuf, slots, wgu, wdn,
-          pa, pb, ra, rb, rc, hid, osend, orecv, pm, up_sum, dn_sum, fin,
-          load_sem, e_send, e_recv, e_own, e_out, sc_sem, t_sem, m_sem, zu_sem, zd_sem, zm_sem, x_sem,
+def layer(dims, rows, exps_in, tok_in, ids_in, probs_in, out, mixed,
+          enc, exps, tok, ids_raw, probs_raw, inv_t, scl_t, s_out, s_in, meta, mix, xcol, m_all, m_send, m_col, sbuf, slots, wgu, wdn,
+          pa, pb, ra, rb, rc, rl, hid, osend, orecv, pm, up_sum, dn_sum, fin,
+          load_sem, in_sem, e_send, e_recv, e_own, sc_sem, t_sem, m_sem, zu_sem, zd_sem, zm_sem, x_sem,
           x_own, a_sem, b_sem, h_sem, i_sem, o_sem, o_own, pu_sem, pd_sem, q_sem):
     nz, nx, ny, fs, unit = dims
     ne, nf = nz * nx, 2 * ny
@@ -36,7 +38,8 @@
     gt, gs = nf * TOK, nf * CAP
     half = nz * gs // 2
     hidden = ne * unit
-    wide_half = fs // 2
+    wide_half = fs // PIECES
+    ring_half = fs // 2
     chunk = half // 2
     experts, span = 2 * ne, unit * nb
     ups, downs = nz // 2, (nz - 1) // 2
@@ -60,23 +63,33 @@
     def at_z(d):
         return lax.rem(z + d + nz, nz)
 
+    small = [local(src, dst, in_sem.at[i]) for i, (src, dst) in enumerate(
+        ((ids_in, ids_raw), (probs_in, probs_raw), (exps_in, exps), (tok_in, tok)))]
+
+    def greet_expert(j):
+        pl.semaphore_signal(barrier, inc=1, device_id={"expert": lax.rem(ex + j, ne)}, device_id_type=MESH)
+
+    def greet_fsdp(j):
+        pl.semaphore_signal(barrier, inc=1, device_id={"fsdp": lax.rem(f + j, nf)}, device_id_type=MESH)
+
+    loop(1, nf, greet_fsdp)
+    loop(1, ne, greet_expert)
+    for copy in small:
+        copy.start()
     for ph, (k, p) in enumerate(PHASES):
         local(rows.at[:, k, p], enc.at[ph], load_sem.at[ph]).start()
 
-    def greet_expert(j):
-        pl.semaphore_signal(barrier, inc=1, device_id={"expert": lax.rem(ex + j, ne)}, device_id_type=MESH)
-
-    def greet_fsdp(j):
-        pl.semaphore_signal(barrier, inc=1, device_id={"fsdp": lax.rem(f + j, nf)}, device_id_type=MESH)
-
-    loop(1, nf, greet_fsdp)
-    loop(1, ne, greet_expert)
-    ids, probs = packed[0:8], packed[8:16]
-    share = probs / jnp.sum(probs, axis=0, keepdims=True)
+    small[0].wait()
+    small[1].wait()
+    top = ids_raw.shape[0]
+    widen_lanes = (lax.broadcasted_iota(jnp.int32, (TOK, 128), 0) == lax.broadcasted_iota(jnp.int32, (TOK, 128), 1)).astype(F32)
+    ids = jnp.dot(ids_raw[...].astype(F32), widen_lanes, precision=lax.Precision.HIGHEST, preferred_element_type=F32)
+    probs = probs_raw[...] / jnp.sum(probs_raw[...], axis=0, keepdims=True)
+    share = jnp.dot(probs, widen_lanes, precision=lax.Precision.HIGHEST, preferred_element_type=F32)
     expert_of = lax.broadcasted_iota(jnp.int32, (experts, 128), 0).astype(F32)
     member = jnp.zeros((experts, 128), F32)
     weight = jnp.zeros((experts, 128), F32)
-    for i in range(8):
+    for i in range(top):
         hit = expert_of == ids[i:i + 1]
         member = member + hit.astype(F32)
         weight = weight + jnp.where(hit, share[i:i + 1], 0.0)
@@ -94,6 +107,7 @@
                 row_list.append(jnp.zeros((8, 128), F32))
     meta[...] = jnp.transpose(jnp.concatenate(row_list, axis=0))[:TOK]
 
+    small[2].wait()
     for p in range(3):
         flat = exps[p].reshape(span, experts).astype(F32)
         if experts < 128:
@@ -142,18 +156,19 @@
 
     def part(n, ref, who):
         ph, lo, width = PARTS[n]
-        return ref.at[ph, who] if width == 2 else ref.at[ph, who, :, pl.ds(lo * wide_half, wide_half)]
+        mine = ref.at[ph] if ref is enc else ref.at[PHASES[ph][0], PHASES[ph][1]]
+        return mine.at[who] if width == PIECES else mine.at[who, :, pl.ds(lo * wide_half, wide_half)]
 
     def elements_some(n, low, high):
         def step(i):
             e = zigzag(i)
-            to_expert(part(n, enc, e), part(n, got, ex), e_send.at[n], e_recv.at[n], e).start()
+            to_expert(part(n, enc, e), part(n, out, ex), e_send.at[n], e_recv.at[n], e).start()
 
         loop(low, high, step)
 
     def elements_send(n):
         elements_some(n, 1, ne)
-        local(part(n, enc, ex), part(n, got, ex), e_own.at[n]).start()
+        local(part(n, enc, ex), part(n, out, ex), e_own.at[n]).start()
 
     def scales_send(i):
         e = zigzag(i)
@@ -161,6 +176,7 @@
 
     encode(0)
     encode(1)
+    small[3].wait()
     pl.semaphore_wait(barrier, ne + nf - 2)
 
     def tok_send(j):
@@ -173,16 +189,16 @@
     loop(1, nf, tok_send)
     local(tok.at[:, pl.ds(pl.multiple_of(f * fs, fs), fs)], xcol.at[z, here], t_sem.at[2]).start()
     local(meta, m_all.at[here], m_sem.at[2]).start()
-    near = NEAR if ne > 16 else 2
+    near = NEAR if ups == 4 else 2
     elements_some(0, 1, near)
-    local(part(0, enc, ex), part(0, got, ex), e_own.at[0]).start()
+    local(part(0, enc, ex), part(0, out, ex), e_own.at[0]).start()
 
     many_f = pl.ds(0, (nf - 1) * TOK)
     local(xcol.at[z, many_f], xcol.at[z, many_f], t_sem.at[1]).wait()
     local(xcol.at[z, here], xcol.at[z, here], t_sem.at[2]).wait()
 
     def cut(h, g):
-        return xcol.at[g, :, pl.ds(h * wide_half, wide_half)]
+        return xcol.at[g, :, pl.ds(h * ring_half, ring_half)]
 
     def push_up(h, step):
         g = at_z(1 - step)
@@ -243,39 +259,36 @@
         if step == max(ups - 1, 1):
             loop(1, ne, scales_send)
             local(s_out.at[ex], s_in.at[ex], sc_sem.at[2]).start()
-            elements_some(0, near, ne)
+        if ups == 4:
+            elements_some(*SLICES[step - 1])
         compact(at_z(-step))
         if step <= downs:
             compact(at_z(step))
 
     local(sbuf.at[x, 0], slots.at[0, x], x_own.at[0]).start()
-    elements_send(1)
+    if ups == 4:
+        elements_some(*SLICES[4])
+        local(part(1, enc, ex), part(1, out, ex), e_own.at[1]).start()
+    else:
+        elements_some(0, near, ne)
+        elements_send(1)
     encode(2)
     elements_send(2)
     for j in range(1, nx):
         to = lax.rem(x + j, nx)
         to_expert(sbuf.at[to, 1], slots.at[1, x], x_sem.at[0, 1], x_sem.at[1, 1], z * nx + to).start()
     local(sbuf.at[x, 1], slots.at[1, x], x_own.at[1]).start()
-    encode(3)
-    elements_send(3)
-    encode(4)
-    elements_send(4)
-    encode(5)
-    for n in range(5, 8):
-        elements_send(n)
+    for ph in range(3, 6):
+        encode(ph)
 
     many_e = pl.ds(0, ne - 1)
     many_x = pl.ds(0, nx - 1)
     many_y = pl.ds(0, ny - 1)
 
     def elements_wait(n):
-        ph, lo, width = PARTS[n]
-        k, p = PHASES[ph]
-        own, all_in = part(n, got, ex), part(n, got, many_e)
+        own, all_in = part(n, out, ex), part(n, out, many_e)
         local(own, own, e_own.at[n]).wait()
         local(all_in, all_in, e_recv.at[n]).wait()
-        if lo + width == 2:
-            local(got.at[ph], out.at[k, p], e_out.at[ph]).start()
 
     def widen(n, dst, base):
         ph, lo, width = PARTS[n]
@@ -287,46 +300,69 @@
             at = pl.multiple_of(i * per * unit, per * unit)
             lines = [jnp.where(diagonal, s_in[i * per + u].astype(F32)[k * 3 + p:k * 3 + p + 1], 0.0) for u in range(per)]
             wide = jnp.dot(jnp.concatenate(lines, axis=0).astype(BF), sel, preferred_element_type=F32)
-            vals = [got[ph, i * per + u, :, pl.ds(lo * wide_half, cols)].astype(F32) * wide[u * unit:(u + 1) * unit] for u in range(per)]
+            vals = [out[k, p, i * per + u, :, pl.ds(lo * wide_half, cols)].astype(F32) * wide[u * unit:(u + 1) * unit] for u in range(per)]
             dst[pl.ds(base + at, per * unit), :] = jnp.concatenate(vals, axis=0).astype(BF)
 
         loop(0, ne // per, step)
 
-    def gate_up(k, c, dst, which):
+    cols = min(256, hidden)
+
+    def gate_up(k, c, dst, which, base):
         lhs = slots[k, :, pl.ds(pl.multiple_of(which * half + c * chunk, chunk), chunk), :].reshape(nx * chunk, fs)
-        cols = min(256, hidden)
 
         def step(n):
-            at = pl.multiple_of(n * cols, cols)
+            at = pl.multiple_of(base + n * cols, cols)
             res = lax.dot_general(lhs, wgu[pl.ds(at, cols), :], (((1,), (1,)), ((), ())), preferred_element_type=F32)
             dst[k, c, :, :, pl.ds(at, cols)] = res.astype(BF).reshape(ny, chunk, cols)
 
-        loop(0, 2 * hidden // cols, step)
-
-    def first_sums(k):
+        loop(0, hidden // cols, step)
+
+    def gates(k):
         elements_wait(2 * k)
         widen(2 * k, wgu, 0)
-        elements_wait(2 * k + 1)
-        widen(2 * k + 1, wgu, hidden)
         local(slots.at[k, many_x], slots.at[k, many_x], x_sem.at[1, k]).wait()
         local(sbuf.at[x, k], slots.at[k, x], x_own.at[k]).wait()
         for c in range(2):
-            gate_up(k, c, pa, 1 - core)
+            gate_up(k, c, pa, 1 - core, 0)
+            gate_up(k, c, pb, core, 0)
+
+    def first_sums(k):
+        elements_wait(2 * k + 1)
+        widen(2 * k + 1, wgu, hidden)
+        for c in range(2):
+            gate_up(k, c, pa, 1 - core, hidden)
             to_fsdp(pa.at[k, c], ra.at[k, c], a_sem.at[0, k, c], a_sem.at[1, k, c], mate).start()
-            gate_up(k, c, pb, core)
+            gate_up(k, c, pb, core, hidden)
         for c in range(2):
             local(pa.at[k, c], ra.at[k, c], a_sem.at[1, k, c]).wait()
-            for j in range(ny):
-                to = lax.rem(y + 1 + j, ny)
+            for j in ((2, 1, 3, 0) if ny == 4 else (1, 0)):
+                to = lax.rem(y + j, ny)
                 rb[k, c, to] = (pb[k, c, to].astype(F32) + ra[k, c, to].astype(F32)).astype(BF)
-                if j < ny - 1:
-                    to_fsdp(rb.at[k, c, to], rc.at[k, c, y], b_sem.at[0, k, c], b_sem.at[1, k, c], to * 2 + core).start()
+                if ny == 4 and j == 2:
+                    for d in range(2):
+                        side = rb.at[k, c, to, :, pl.ds(d * hidden, hidden)]
+                        to_fsdp(side, rl.at[k, c, d], b_sem.at[0, k, c, d], b_sem.at[1, k, c, d], beside(d)).start()
+            if ny != 4:
+                to_fsdp(rb.at[k, c, 1 - y], rc.at[k, c, 0], b_sem.at[0, k, c, 2], b_sem.at[1, k, c, 2], (1 - y) * 2 + core).start()
+
+    def beside(d):
+        return lax.rem(y + (1 if d == 0 else ny - 1), ny) * 2 + core
+
+    def relay(k, c):
+        if ny != 4:
+            return
+        for d in range(2):
+            local(rl.at[k, c, d], rl.at[k, c, d], b_sem.at[1, k, c, d]).wait()
+            to = lax.rem(y + (1 if d == 0 else ny - 1), ny)
+            side = pl.ds(d * hidden, hidden)
+            rb[k, c, to, :, side] = (rb[k, c, to, :, side].astype(F32) + rl[k, c, d].astype(F32)).astype(BF)
+            to_fsdp(rb.at[k, c, to], rc.at[k, c, d], b_sem.at[0, k, c, 2 + d], b_sem.at[1, k, c, 2 + d], beside(d)).start()
 
     def activate(k, c):
-        local(rc.at[k, c, many_y], rc.at[k, c, many_y], b_sem.at[1, k, c]).wait()
         total = rb[k, c, y].astype(F32)
-        for j in range(1, ny):
-            total = total + rc[k, c, lax.rem(y + j, ny)].astype(F32)
+        for d in range(2 if ny == 4 else 1):
+            local(rc.at[k, c, d], rc.at[k, c, d], b_sem.at[1, k, c, 2 + d]).wait()
+            total = total + rc[k, c, d].astype(F32)
         gate, up = total[:, :hidden], total[:, hidden:]
         hid[k, c, core, y] = (gate / (1.0 + jnp.exp(-gate)) * up).astype(BF)
         for j in range(1, ny):
@@ -370,9 +406,13 @@
         res = lax.dot_general(hi, vals, both, preferred_element_type=F32)
         return res + lax.dot_general(lo, vals, both, preferred_element_type=F32)
 
+    def blend_rest(h):
+        for d in range(nz):
+            if d not in (ups, downs + 2):
+                mix[h, d] = blend(h, at_z(d))
+
     def sum_up(h, step):
-        g = at_z(ups + 1 - step)
-        val = blend(h, g)
+        val = mix[h, ups + 1 - step]
         if step > 1:
             local(up_sum.at[h, 0], up_sum.at[h, 0], pu_sem.at[1, h, step - 2]).wait()
             val = val + up_sum[h, step - 2].astype(F32)
@@ -380,8 +420,7 @@
         to_expert(pm.at[h, 0, step - 1], up_sum.at[h, step - 1], pu_sem.at[0, h, step - 1], pu_sem.at[1, h, step - 1], at_z(1) * nx + x).start()
 
     def sum_down(h, step):
-        g = at_z(step - downs - 1)
-        val = blend(h, g)
+        val = mix[h, nz + step - downs - 1]
         if step > 1:
             local(dn_sum.at[h, 0], dn_sum.at[h, 0], pd_sem.at[1, h, step - 2]).wait()
             val = val + dn_sum[h, step - 2].astype(F32)
@@ -394,7 +433,7 @@
             sum_down(h, step)
 
     def finish(h):
-        val = blend(h, z)
+        val = mix[h, 0]
         local(up_sum.at[h, 0], up_sum.at[h, 0], pu_sem.at[1, h, ups - 1]).wait()
         val = val + up_sum[h, ups - 1].astype(F32)
         if downs:
@@ -413,50 +452,61 @@
     local(s_in.at[many_e], s_in.at[many_e], sc_sem.at[1]).wait()
     local(s_out.at[ex], s_in.at[ex], sc_sem.at[2]).wait()
 
+    gates(0)
+    elements_send(3)
     first_sums(0)
-    for c in range(2):
-        activate(0, c)
+    relay(0, 0)
+    relay(0, 1)
+    gates(1)
+    for n in range(4, 4 + PIECES):
+        elements_send(n)
+    activate(0, 0)
+    activate(0, 1)
+    first_sums(1)
+    for n in range(4 + PIECES, len(PARTS)):
+        elements_send(n)
     for c in range(2):
         forward(0, c)
-    first_sums(1)
-    elements_wait(4)
-    widen(4, wdn.at[0], 0)
-    for c in range(2):
-        hidden_wait(0, c)
-        down(0, 0, c)
-    activate(1, 0)
-    elements_wait(6)
-    widen(6, wdn.at[1], 0)
-    for c in range(2):
-        down(0, 1, c)
+    relay(1, 0)
+    relay(1, 1)
+    for h in range(PIECES):
+        elements_wait(4 + h)
+        widen(4 + h, wdn.at[h], 0)
+        for c in range(2):
+            if h == 0:
+                hidden_wait(0, c)
+            down(0, h, c)
+        if h == 0:
+            activate(1, 0)
     activate(1, 1)
     forward(1, 0)
-    elements_wait(5)
-    widen(5, wdn.at[0], 0)
-    hidden_wait(1, 0)
-    down(1, 0, 0)
-    elements_wait(7)
-    widen(7, wdn.at[1], 0)
-    down(1, 1, 0)
-    forward(1, 1)
-    hidden_wait(1, 1)
-    down(1, 0, 1)
-    down(1, 1, 1)
-    outputs_wait(0)
-    ring(0, 1)
-    outputs_wait(1)
-    for step in range(1, ups + 1):
-        ring(1, step)
-        if step < ups:
-            ring(0, step + 1)
-    finish(0)
-    finish(1)
-
-    for n in range(8):
+    for h in range(PIECES):
+        elements_wait(4 + PIECES + h)
+        widen(4 + PIECES + h, wdn.at[h], 0)
+        if h == 0:
+            hidden_wait(1, 0)
+        down(1, h, 0)
+        if h == 0:
+            forward(1, 1)
+            hidden_wait(1, 1)
+        down(1, h, 1)
+    for t in range(PIECES + ups):
+        for h in range(PIECES):
+            step = t - h + 1
+            if step == 1:
+                outputs_wait(h)
+                for d in (ups, downs + 2) if downs else (ups,):
+                    mix[h, d] = blend(h, at_z(d))
+            if 1 <= step <= ups:
+                ring(h, step)
+            if step == 1:
+                blend_rest(h)
+            if step == ups + 1:
+                finish(h)
+
+    for n in range(len(PARTS)):
         out_n = part(n, enc, many_e)
         local(out_n, out_n, e_send.at[n]).wait()
-    for ph, (k, p) in enumerate(PHASES):
-        local(got.at[ph], out.at[k, p], e_out.at[ph]).wait()
     local(s_in.at[many_e], s_in.at[many_e], sc_sem.at[0]).wait()
     local(xcol.at[z, many_f], xcol.at[z, many_f], t_sem.at[0]).wait()
     local(m_all.at[many_f], m_all.at[many_f], m_sem.at[0]).wait()
@@ -470,10 +520,13 @@
         local(slots.at[k, many_x], slots.at[k, many_x], x_sem.at[0, k]).wait()
         for c in range(2):
             local(pa.at[k, c], pa.at[k, c], a_sem.at[0, k, c]).wait()
-            local(rc.at[k, c, many_y], rc.at[k, c, many_y], b_sem.at[0, k, c]).wait()
+            for d in range(2 if ny == 4 else 1):
+                local(rc.at[k, c, d], rc.at[k, c, d], b_sem.at[0, k, c, 2 + d]).wait()
+                if ny == 4:
+                    local(rl.at[k, c, d], rl.at[k, c, d], b_sem.at[0, k, c, d]).wait()
             local(hid.at[k, c, 0, many_y], hid.at[k, c, 0, many_y], h_sem.at[0, k, c]).wait()
             local(hid.at[k, c, 0], hid.at[k, c, 0], i_sem.at[0, k, c]).wait()
-    for h in range(2):
+    for h in range(PIECES):
         for k in range(2):
             for c in range(2):
                 local(orecv.at[h, k, c, many_x], orecv.at[h, k, c, many_x], o_sem.at[0, h, k, c]).wait()
@@ -488,46 +541,44 @@
         local(rest, rest, q_sem.at[0, h]).wait()
 
 
-def run_layer(dims, rows, exps, tok, packed):
+def run_layer(dims, rows, exps, tok, ids, probs):
     nz, nx, ny, fs, unit = dims
     ne, nf = nz * nx, 2 * ny
     gt, gs = nf * TOK, nf * CAP
     half, hidden, ups = nz * gs // 2, ne * unit, nz // 2
-    chunk, hw, span = half // 2, fs // 2, unit * (fs // BLOCK)
+    chunk, hw, span = half // 2, fs // PIECES, unit * (fs // BLOCK)
+    np = len(PARTS)
     vm = pl.BlockSpec(memory_space=pltpu.VMEM)
-    hbm = pl.BlockSpec(memory_space=pl.ANY)
+    hbm = pl.BlockSpec(memory_space=pltpu.HBM)
+    anywhere = pl.BlockSpec(memory_space=pl.ANY)
     V = lambda *s: pltpu.VMEM(s, BF)
     W = lambda *s: pltpu.VMEM(s, F32)
     dma = lambda *s: pltpu.SemaphoreType.DMA(s)
-    sums = [V(2, 2, ny, chunk, 2 * hidden)] * 5
+    sums = [V(2, 2, ny, chunk, 2 * hidden)] * 4 + [V(2, 2, 2, chunk, 2 * hidden), V(2, 2, 2, chunk, hidden)]
     return pl.pallas_call(
         functools.partial(layer, dims),
         out_shape=(jax.ShapeDtypeStruct((2, 3, ne, unit, fs), BF), jax.ShapeDtypeStruct((TOK, nf * fs), BF)),
-        in_specs=[hbm, vm, vm, vm],
-        out_specs=(hbm, vm),
+        in_specs=[hbm] * 5,
+        out_specs=(vm, anywhere),
         scratch_shapes=[
-            V(6, ne, unit, fs), V(6, ne, unit, fs), W(3, 2 * ne, span), W(3, 2 * ne, span), V(ne, 8, span), V(ne, 8, span),
-            W(TOK, 128), V(nz, gt, fs), W(gt, 128), W(nz, 16, gt), W(nz, 16, gt),
-            V(nx, 2, nz * gs, fs), V(2, nx, nz * gs, fs), V(2 * hidden, fs), V(2, hidden, hw),
+            V(6, ne, unit, fs), pltpu.VMEM(exps.shape, jnp.int32), V(TOK, nf * fs), pltpu.VMEM(ids.shape, jnp.int32), W(*probs.shape), W(3, 2 * ne, span), W(3, 2 * ne, span), V(ne, 8, span), V(ne, 8, span),
+            W(TOK, 128), W(PIECES, nz, gt, hw), V(nz, gt, fs), W(gt, 128), W(nz, 16, gt), W(nz, 16, gt),
+            V(nx, 2, nz * gs, fs), V(2, nx, nz * gs, fs), V(2 * hidden, fs), V(PIECES, hidden, hw),
             *sums,
-            V(2, 2, 2, ny, chunk, hidden), V(2, 2, 2, nx, 2 * chunk, hw), V(2, 2, 2, nx, 2 * chunk, hw),
-            V(2, 2, ups, gt, hw), V(2, ups, gt, hw), V(2, ups, gt, hw), V(2, gt, hw),
-            dma(6), dma(8), dma(8), dma(8), dma(6), dma(3), dma(3), dma(3), dma(2, 2, ups), dma(2, 2, ups), dma(3), dma(2, 2), dma(2),
-            dma(2, 2, 2), dma(2, 2, 2), dma(2, 2, 2), dma(2, 2, 2), dma(2, 2, 2, 2), dma(2, 2, 2), dma(2, 2, ups), dma(2, 2, ups), dma(3, 2),
+            V(2, 2, 2, ny, chunk, hidden), V(PIECES, 2, 2, nx, 2 * chunk, hw), V(PIECES, 2, 2, nx, 2 * chunk, hw),
+            V(PIECES, 2, ups, gt, hw), V(PIECES, ups, gt, hw), V(PIECES, ups, gt, hw), V(PIECES, gt, hw),
+            dma(6), dma(4), dma(np), dma(np), dma(np), dma(3), dma(3), dma(3), dma(2, 2, ups), dma(2, 2, ups), dma(3), dma(2, 2), dma(2),
+            dma(2, 2, 2), dma(2, 2, 2, 4), dma(2, 2, 2), dma(2, 2, 2), dma(2, PIECES, 2, 2), dma(PIECES, 2, 2), dma(2, PIECES, ups), dma(2, PIECES, ups), dma(3, PIECES),
         ],
         compiler_params=pltpu.CompilerParams(collective_id=1, has_side_effects=True, vmem_limit_bytes=VMEM_LIMIT),
         name="layer",
-    )(rows, exps, tok, packed)
+    )(rows, exps, tok, ids, probs)
 
 
 def body(dims, tokens, learner_rows, exponents, expert_ids, route_probs):
     nz, nx, ny, fs, unit = dims
     ne = nz * nx
-    top = expert_ids.shape[1]
-    ids = jnp.pad(expert_ids.T.astype(F32), ((0, 8 - top), (0, 128 - TOK)), constant_values=-1.0)
-    probs = jnp.pad(jnp.pad(route_probs.T, ((0, 8 - top), (0, 0))), ((0, 0), (0, 128 - TOK)), constant_values=1.0)
-    packed = jnp.concatenate([ids, probs], axis=0)
-    el, mixed = run_layer(dims, learner_rows.reshape(ne, 2, 3, unit, fs), exponents.transpose(1, 2, 3, 0), tokens, packed)
+    el, mixed = run_layer(dims, learner_rows.reshape(ne, 2, 3, unit, fs), exponents.transpose(1, 2, 3, 0), tokens, expert_ids.T, route_probs.T)
     return el.reshape(2, 3, ne * unit, fs), mixed
 
 

time: 185 us -> 175 us (0.946)
  Pallas kernels: 176 us -> 168 us
  other arithmetic: 1.98 us -> 0 us
    pallas_call x1, Pallas kernels: 176 us -> 168 us  [run_layer(): pl.pallas_call(functools.partial(layer, dims), out_shape=(jax.ShapeDtypeS...]
    unnamed x4 -> x10, local copies, waits for them, and re-layouts: 5.81 us -> 6.18 us
where the time goes in v4:
time: 175 us
  Pallas kernels  168 us (96%)
  local copies, waits for them, and re-layouts  6.18 us (4%)
    pallas_call x1, Pallas kernels, run_layer(): pl.pallas_call(functools.partial(layer, dims), out_shape=(jax.ShapeDtypeS...  168 us
    unnamed x10, local copies, waits for them, and re-layouts  6.18 us

profile of v4, /device:TPU:1, one launch (start us, length us, event | category | flops | bytes accessed | tf_op | source)
XLA Modules:
  0.0 175.0 jit_solution(18029900726004640634)
XLA Ops:
  0.6 0.0 copy-start
  0.6 1.1 copy-done
  1.7 0.0 copy-start.1
  1.7 0.9 copy-done.1
  2.6 0.0 copy-start.2
  2.6 0.7 copy-done.2
  3.3 0.0 copy-start.3
  3.3 0.7 copy-done.3
  4.0 168.1 %layer.1 = (bf16[2,3,32,24,512]{4,3,2,1,0:T(8,128)(2,1)S(1)}, bf16[16,4096]{1,0:T(8,128)(2,1)S(1)}) custom-call(bf16[32,2,3,24,512]{4,3,2,1,0:T(8,128)(2,1)} %bitcast.9, s32[3,24,16,64]{3,2,1,0:T(8,128)S(1)} %bitcast.6, bf16[16,4096]{1,0:T(8,128)(2,1)S(1)} %copy-done.1, s32[8,16]{1,0:T(8,128)S(1)} %bitcast.7, f32[8,16]{1,0:T(8,128)S(1)} %bitcast.8), custom_call_target="tpu_custom_call" | custom-call | tf_op jit(solution)/shard_map/layer/pallas_call | solution.py:558
  172.1 2.2 %copy.9 = bf16[2,3,768,512]{3,2,1,0:T(8,128)(2,1)} copy(bf16[2,3,768,512]{3,2,1,0:T(8,128)(2,1)S(1)} %bitcast.5) | data formatting | bytes 9437184
  174.3 0.7 copy.10
Async XLA Ops:
  0.6 1.1 copy-start
  1.7 0.9 copy-start.1
  2.6 0.7 copy-start.2
  3.3 0.7 copy-start.3

commit v5 on v4

--- a/solution.py
+++ b/solution.py
@@ -9,14 +9,16 @@
 BLOCK = 32
 CAP = 4
 NEAR = 20
-SLICES = ((0, 20, 26), (0, 26, 32), (1, 1, 16), (1, 16, 24), (1, 24, 32))
+SLICES = ((0, 20, 32), (1, 1, 20), (1, 20, 32), (2, 1, 20), (2, 20, 32))
+ROWS = ((0, 16), (16, 8))
 VMEM_LIMIT = 47 * 1024 * 1024
 TOK = 16
 MESH = pl.DeviceIdType.MESH
 BF, F32 = jnp.bfloat16, jnp.float32
 PHASES = ((0, 0), (0, 1), (1, 0), (1, 1), (0, 2), (1, 2))
 PIECES = 2
-PARTS = tuple((ph, 0, PIECES) for ph in range(4)) + tuple((ph, h, 1) for ph in (4, 5) for h in range(PIECES))
+PARTS = tuple((2 * k + p, *ROWS[u], 0, PIECES) for k in range(2) for u in range(2) for p in range(2)) + tuple(
+    (4 + k, 0, 24, h, 1) for h in range(PIECES) for k in range(2))
 
 
 def loop(low, high, step):
@@ -40,7 +42,8 @@
     hidden = ne * unit
     wide_half = fs // PIECES
     ring_half = fs // 2
-    chunk = half // 2
+    sizes = tuple(ne * n for _, n in ROWS)
+    starts = (0, sizes[0])
     experts, span = 2 * ne, unit * nb
     ups, downs = nz // 2, (nz - 1) // 2
     ex, f = lax.axis_index("expert"), lax.axis_index("fsdp")
@@ -155,9 +158,9 @@
         return lax.rem(ex + jnp.where(lax.rem(i, 2) == 1, (i + 1) // 2, ne - i // 2), ne)
 
     def part(n, ref, who):
-        ph, lo, width = PARTS[n]
+        ph, row, count, lo, width = PARTS[n]
         mine = ref.at[ph] if ref is enc else ref.at[PHASES[ph][0], PHASES[ph][1]]
-        return mine.at[who] if width == PIECES else mine.at[who, :, pl.ds(lo * wide_half, wide_half)]
+        return mine.at[who, pl.ds(row, count), pl.ds(lo * wide_half, width * wide_half)]
 
     def elements_some(n, low, high):
         def step(i):
@@ -268,12 +271,15 @@
     local(sbuf.at[x, 0], slots.at[0, x], x_own.at[0]).start()
     if ups == 4:
         elements_some(*SLICES[4])
-        local(part(1, enc, ex), part(1, out, ex), e_own.at[1]).start()
+        for n in (1, 2):
+            local(part(n, enc, ex), part(n, out, ex), e_own.at[n]).start()
     else:
         elements_some(0, near, ne)
         elements_send(1)
+        elements_send(2)
+    elements_send(3)
     encode(2)
-    elements_send(2)
+    elements_send(4)
     for j in range(1, nx):
         to = lax.rem(x + j, nx)
         to_expert(sbuf.at[to, 1], slots.at[1, x], x_sem.at[0, 1], x_sem.at[1, 1], z * nx + to).start()
@@ -291,106 +297,116 @@
         local(all_in, all_in, e_recv.at[n]).wait()
 
     def widen(n, dst, base):
-        ph, lo, width = PARTS[n]
+        ph, row, count, lo, width = PARTS[n]
         k, p = PHASES[ph]
         cols = width * wide_half
         sel = pick(lo * wide_half, cols)
 
         def step(i):
-            at = pl.multiple_of(i * per * unit, per * unit)
-            lines = [jnp.where(diagonal, s_in[i * per + u].astype(F32)[k * 3 + p:k * 3 + p + 1], 0.0) for u in range(per)]
+            lines = [jnp.where(diagonal, s_in[i * per + u].astype(F32)[k * 3 + p:k * 3 + p + 1], 0.0)[row:row + count] for u in range(per)]
             wide = jnp.dot(jnp.concatenate(lines, axis=0).astype(BF), sel, preferred_element_type=F32)
-            vals = [out[k, p, i * per + u, :, pl.ds(lo * wide_half, cols)].astype(F32) * wide[u * unit:(u + 1) * unit] for u in range(per)]
-            dst[pl.ds(base + at, per * unit), :] = jnp.concatenate(vals, axis=0).astype(BF)
+            vals = [out[k, p, i * per + u, pl.ds(row, count), pl.ds(lo * wide_half, cols)].astype(F32) * wide[u * count:(u + 1) * count] for u in range(per)]
+            if count < unit:
+                at = pl.multiple_of(base + i * per * count, per * count)
+                dst[pl.ds(at, per * count), :] = jnp.concatenate(vals, axis=0).astype(BF)
+            else:
+                for (r, m), start in zip(ROWS, starts):
+                    at = pl.multiple_of(start + i * per * m, per * m)
+                    dst[pl.ds(at, per * m), :] = jnp.concatenate([v[r:r + m] for v in vals], axis=0).astype(BF)
 
         loop(0, ne // per, step)
 
-    cols = min(256, hidden)
-
-    def gate_up(k, c, dst, which, base):
-        lhs = slots[k, :, pl.ds(pl.multiple_of(which * half + c * chunk, chunk), chunk), :].reshape(nx * chunk, fs)
+    def gate_up(k, u, dst, which):
+        lhs = slots[k, :, pl.ds(pl.multiple_of(which * half, half), half), :].reshape(nx * half, fs)
+        cols = min(256, sizes[u])
 
         def step(n):
-            at = pl.multiple_of(base + n * cols, cols)
+            at = pl.multiple_of(2 * starts[u] + n * cols, cols)
             res = lax.dot_general(lhs, wgu[pl.ds(at, cols), :], (((1,), (1,)), ((), ())), preferred_element_type=F32)
-            dst[k, c, :, :, pl.ds(at, cols)] = res.astype(BF).reshape(ny, chunk, cols)
-
-        loop(0, hidden // cols, step)
-
-    def gates(k):
-        elements_wait(2 * k)
-        widen(2 * k, wgu, 0)
-        local(slots.at[k, many_x], slots.at[k, many_x], x_sem.at[1, k]).wait()
-        local(sbuf.at[x, k], slots.at[k, x], x_own.at[k]).wait()
-        for c in range(2):
-            gate_up(k, c, pa, 1 - core, 0)
-            gate_up(k, c, pb, core, 0)
-
-    def first_sums(k):
-        elements_wait(2 * k + 1)
-        widen(2 * k + 1, wgu, hidden)
-        for c in range(2):
-            gate_up(k, c, pa, 1 - core, hidden)
-            to_fsdp(pa.at[k, c], ra.at[k, c], a_sem.at[0, k, c], a_sem.at[1, k, c], mate).start()
-            gate_up(k, c, pb, core, hidden)
-        for c in range(2):
-            local(pa.at[k, c], ra.at[k, c], a_sem.at[1, k, c]).wait()
-            for j in ((2, 1, 3, 0) if ny == 4 else (1, 0)):
-                to = lax.rem(y + j, ny)
-                rb[k, c, to] = (pb[k, c, to].astype(F32) + ra[k, c, to].astype(F32)).astype(BF)
-                if ny == 4 and j == 2:
-                    for d in range(2):
-                        side = rb.at[k, c, to, :, pl.ds(d * hidden, hidden)]
-                        to_fsdp(side, rl.at[k, c, d], b_sem.at[0, k, c, d], b_sem.at[1, k, c, d], beside(d)).start()
-            if ny != 4:
-                to_fsdp(rb.at[k, c, 1 - y], rc.at[k, c, 0], b_sem.at[0, k, c, 2], b_sem.at[1, k, c, 2], (1 - y) * 2 + core).start()
+            dst[k, :, :, pl.ds(at, cols)] = res.astype(BF).reshape(ny, half, cols)
+
+        loop(0, 2 * sizes[u] // cols, step)
+
+    def both(u):
+        return pl.ds(2 * starts[u], 2 * sizes[u])
+
+    def first_sums(k, u):
+        if u == 0:
+            local(slots.at[k, many_x], slots.at[k, many_x], x_sem.at[1, k]).wait()
+            local(sbuf.at[x, k], slots.at[k, x], x_own.at[k]).wait()
+        for p in range(2):
+            elements_wait(4 * k + 2 * u + p)
+            widen(4 * k + 2 * u + p, wgu, 2 * starts[u] + p * sizes[u])
+        gate_up(k, u, pa, 1 - core)
+        to_fsdp(pa.at[k, :, :, both(u)], ra.at[k, :, :, both(u)], a_sem.at[0, k, u], a_sem.at[1, k, u], mate).start()
+        gate_up(k, u, pb, core)
+        local(pa.at[k, :, :, both(u)], ra.at[k, :, :, both(u)], a_sem.at[1, k, u]).wait()
+        for j in ((2, 1, 3, 0) if ny == 4 else (1, 0)):
+            to = lax.rem(y + j, ny)
+            rb[k, to, :, both(u)] = (pb[k, to, :, both(u)].astype(F32) + ra[k, to, :, both(u)].astype(F32)).astype(BF)
+            if ny == 4 and j == 2:
+                for d in range(2):
+                    side = rb.at[k, to, :, pl.ds(2 * starts[u] + d * sizes[u], sizes[u])]
+                    to_fsdp(side, passed(rl, k, u, d), b_sem.at[0, k, u, d], b_sem.at[1, k, u, d], beside(d)).start()
+        if ny != 4:
+            to_fsdp(rb.at[k, 1 - y, :, both(u)], rc.at[k, 0, :, both(u)], b_sem.at[0, k, u, 2], b_sem.at[1, k, u, 2], (1 - y) * 2 + core).start()
+
+    def passed(ref, k, u, d):
+        return ref.at[k, d, :, pl.ds(starts[u], sizes[u])]
 
     def beside(d):
         return lax.rem(y + (1 if d == 0 else ny - 1), ny) * 2 + core
 
-    def relay(k, c):
+    def relay(k, u):
         if ny != 4:
             return
         for d in range(2):
-            local(rl.at[k, c, d], rl.at[k, c, d], b_sem.at[1, k, c, d]).wait()
+            local(passed(rl, k, u, d), passed(rl, k, u, d), b_sem.at[1, k, u, d]).wait()
             to = lax.rem(y + (1 if d == 0 else ny - 1), ny)
-            side = pl.ds(d * hidden, hidden)
-            rb[k, c, to, :, side] = (rb[k, c, to, :, side].astype(F32) + rl[k, c, d].astype(F32)).astype(BF)
-            to_fsdp(rb.at[k, c, to], rc.at[k, c, d], b_sem.at[0, k, c, 2 + d], b_sem.at[1, k, c, 2 + d], beside(d)).start()
-
-    def activate(k, c):
-        total = rb[k, c, y].astype(F32)
+            side = pl.ds(2 * starts[u] + d * sizes[u], sizes[u])
+            rb[k, to, :, side] = (rb[k, to, :, side].astype(F32) + rl[k, d, :, pl.ds(starts[u], sizes[u])].astype(F32)).astype(BF)
+            to_fsdp(rb.at[k, to, :, both(u)], rc.at[k, d, :, both(u)], b_sem.at[0, k, u, 2 + d], b_sem.at[1, k, u, 2 + d], beside(d)).start()
+
+    def units(u):
+        return pl.ds(starts[u], sizes[u])
+
+    def activate(k, u):
+        total = rb[k, y, :, both(u)].astype(F32)
         for d in range(2 if ny == 4 else 1):
-            local(rc.at[k, c, d], rc.at[k, c, d], b_sem.at[1, k, c, 2 + d]).wait()
-            total = total + rc[k, c, d].astype(F32)
-        gate, up = total[:, :hidden], total[:, hidden:]
-        hid[k, c, core, y] = (gate / (1.0 + jnp.exp(-gate)) * up).astype(BF)
+            local(rc.at[k, d, :, both(u)], rc.at[k, d, :, both(u)], b_sem.at[1, k, u, 2 + d]).wait()
+            total = total + rc[k, d, :, both(u)].astype(F32)
+        gate, up = total[:, :sizes[u]], total[:, sizes[u]:]
+        hid[k, core, y, :, units(u)] = (gate / (1.0 + jnp.exp(-gate)) * up).astype(BF)
         for j in range(1, ny):
             to = lax.rem(y + j, ny)
-            to_fsdp(hid.at[k, c, core, y], hid.at[k, c, core, y], h_sem.at[0, k, c], h_sem.at[1, k, c], to * 2 + core).start()
-
-    def forward(k, c):
-        local(hid.at[k, c, 0, many_y], hid.at[k, c, 0, many_y], h_sem.at[1, k, c]).wait()
-        to_fsdp(hid.at[k, c, core], hid.at[k, c, core], i_sem.at[0, k, c], i_sem.at[1, k, c], mate).start()
-
-    def hidden_wait(k, c):
-        local(hid.at[k, c, 0], hid.at[k, c, 0], i_sem.at[1, k, c]).wait()
-
-    def down(k, h, c):
+            mine = hid.at[k, core, y, :, units(u)]
+            to_fsdp(mine, mine, h_sem.at[0, k, u], h_sem.at[1, k, u], to * 2 + core).start()
+
+    def forward(k, u):
+        some = hid.at[k, 0, many_y, :, units(u)]
+        local(some, some, h_sem.at[1, k, u]).wait()
+        mine = hid.at[k, core, :, :, units(u)]
+        to_fsdp(mine, mine, i_sem.at[0, k, u], i_sem.at[1, k, u], mate).start()
+
+    def hidden_wait(k):
+        for u in range(2):
+            some = hid.at[k, 0, :, :, units(u)]
+            local(some, some, i_sem.at[1, k, u]).wait()
+
+    def down(k, h):
         for j in range(nx):
             to = lax.rem(x + 1 + j, nx)
-            lhs = jnp.concatenate([hid[k, c, 0, to], hid[k, c, 1, to]], axis=0)
-            osend[h, k, c, to] = jnp.dot(lhs, wdn[h], preferred_element_type=F32).astype(BF)
+            lhs = jnp.concatenate([hid[k, 0, to], hid[k, 1, to]], axis=0)
+            osend[h, k, to] = jnp.dot(lhs, wdn[...], preferred_element_type=F32).astype(BF)
             if j < nx - 1:
-                to_expert(osend.at[h, k, c, to], orecv.at[h, k, c, x], o_sem.at[0, h, k, c], o_sem.at[1, h, k, c], z * nx + to).start()
+                to_expert(osend.at[h, k, to], orecv.at[h, k, x], o_sem.at[0, h, k], o_sem.at[1, h, k], z * nx + to).start()
             else:
-                local(osend.at[h, k, c, to], orecv.at[h, k, c, to], o_own.at[h, k, c]).start()
+                local(osend.at[h, k, to], orecv.at[h, k, to], o_own.at[h, k]).start()
 
     def outputs_wait(h):
         for k in range(2):
-            for c in range(2):
-                local(orecv.at[h, k, c, many_x], orecv.at[h, k, c, many_x], o_sem.at[1, h, k, c]).wait()
-                local(osend.at[h, k, c, x], orecv.at[h, k, c, x], o_own.at[h, k, c]).wait()
+            local(orecv.at[h, k, many_x], orecv.at[h, k, many_x], o_sem.at[1, h, k]).wait()
+            local(osend.at[h, k, x], orecv.at[h, k, x], o_own.at[h, k]).wait()
 
     def blend(h, g):
         tgt = targets(g)
@@ -398,13 +414,11 @@
         hot = jnp.concatenate([jnp.where(slot_of == tgt[i:i + 1], share[i:i + 1], 0.0) for i in range(2 * nx)], axis=0)
         hi = hot.astype(BF)
         lo = (hot - hi.astype(F32)).astype(BF)
-        which, inside = g // (nz // 2), lax.rem(g, nz // 2) * gs
-        c, spot = inside // chunk, lax.rem(inside, chunk)
-        at = pl.ds(pl.multiple_of(which * chunk + spot, gs), gs)
-        vals = jnp.concatenate([orecv[h, i % 2, c, i // 2, at, :] for i in range(2 * nx)], axis=0)
-        both = (((0,), (0,)), ((), ()))
-        res = lax.dot_general(hi, vals, both, preferred_element_type=F32)
-        return res + lax.dot_general(lo, vals, both, preferred_element_type=F32)
+        at = pl.ds(pl.multiple_of(g * gs, gs), gs)
+        vals = jnp.concatenate([orecv[h, i % 2, i // 2, at, :] for i in range(2 * nx)], axis=0)
+        rows_of = (((0,), (0,)), ((), ()))
+        res = lax.dot_general(hi, vals, rows_of, preferred_element_type=F32)
+        return res + lax.dot_general(lo, vals, rows_of, preferred_element_type=F32)
 
     def blend_rest(h):
         for d in range(nz):
@@ -452,57 +466,60 @@
     local(s_in.at[many_e], s_in.at[many_e], sc_sem.at[1]).wait()
     local(s_out.at[ex], s_in.at[ex], sc_sem.at[2]).wait()
 
-    gates(0)
-    elements_send(3)
-    first_sums(0)
+    def last(n, k, h):
+        elements_wait(n)
+        widen(n, wdn, 0)
+        if h == 0:
+            hidden_wait(k)
+        down(k, h)
+
+    def begin(h):
+        outputs_wait(h)
+        for d in (ups, downs + 2) if downs else (ups,):
+            mix[h, d] = blend(h, at_z(d))
+        ring(h, 1)
+        blend_rest(h)
+
+    first_sums(0, 0)
+    elements_send(5)
+    first_sums(0, 1)
     relay(0, 0)
+    elements_send(6)
+    elements_send(7)
     relay(0, 1)
-    gates(1)
-    for n in range(4, 4 + PIECES):
-        elements_send(n)
     activate(0, 0)
     activate(0, 1)
-    first_sums(1)
-    for n in range(4 + PIECES, len(PARTS)):
-        elements_send(n)
-    for c in range(2):
-        forward(0, c)
+    elements_send(8)
+    first_sums(1, 0)
+    forward(0, 0)
+    forward(0, 1)
+    elements_send(9)
     relay(1, 0)
+    first_sums(1, 1)
+    elements_send(10)
+    elements_send(11)
+    activate(1, 0)
     relay(1, 1)
-    for h in range(PIECES):
-        elements_wait(4 + h)
-        widen(4 + h, wdn.at[h], 0)
-        for c in range(2):
-            if h == 0:
-                hidden_wait(0, c)
-            down(0, h, c)
-        if h == 0:
-            activate(1, 0)
+    last(8, 0, 0)
     activate(1, 1)
     forward(1, 0)
-    for h in range(PIECES):
-        elements_wait(4 + PIECES + h)
-        widen(4 + PIECES + h, wdn.at[h], 0)
-        if h == 0:
-            hidden_wait(1, 0)
-        down(1, h, 0)
-        if h == 0:
-            forward(1, 1)
-            hidden_wait(1, 1)
-        down(1, h, 1)
-    for t in range(PIECES + ups):
-        for h in range(PIECES):
-            step = t - h + 1
-            if step == 1:
-                outputs_wait(h)
-                for d in (ups, downs + 2) if downs else (ups,):
-                    mix[h, d] = blend(h, at_z(d))
-            if 1 <= step <= ups:
-                ring(h, step)
-            if step == 1:
-                blend_rest(h)
-            if step == ups + 1:
-                finish(h)
+    forward(1, 1)
+    last(9, 1, 0)
+    last(10, 0, 1)
+    begin(0)
+    last(11, 1, 1)
+    for step in range(2, ups):
+        ring(0, step)
+    begin(1)
+    if ups > 1:
+        ring(0, ups)
+    for step in range(2, ups + 1):
+        ring(1, step)
+        if step == min(3, ups):
+            finish(0)
+    if ups == 1:
+        finish(0)
+    finish(1)
 
     for n in range(len(PARTS)):
         out_n = part(n, enc, many_e)
@@ -518,18 +535,18 @@
     local(m_col.at[many_z], m_col.at[many_z], zm_sem.at[0]).wait()
     for k in range(2):
         local(slots.at[k, many_x], slots.at[k, many_x], x_sem.at[0, k]).wait()
-        for c in range(2):
-            local(pa.at[k, c], pa.at[k, c], a_sem.at[0, k, c]).wait()
+        for u in range(2):
+            local(pa.at[k, :, :, both(u)], pa.at[k, :, :, both(u)], a_sem.at[0, k, u]).wait()
             for d in range(2 if ny == 4 else 1):
-                local(rc.at[k, c, d], rc.at[k, c, d], b_sem.at[0, k, c, 2 + d]).wait()
+                local(rc.at[k, d, :, both(u)], rc.at[k, d, :, both(u)], b_sem.at[0, k, u, 2 + d]).wait()
                 if ny == 4:
-                    local(rl.at[k, c, d], rl.at[k, c, d], b_sem.at[0, k, c, d]).wait()
-            local(hid.at[k, c, 0, many_y], hid.at[k, c, 0, many_y], h_sem.at[0, k, c]).wait()
-            local(hid.at[k, c, 0], hid.at[k, c, 0], i_sem.at[0, k, c]).wait()
+                    local(passed(rl, k, u, d), passed(rl, k, u, d), b_sem.at[0, k, u, d]).wait()
+            some, full = hid.at[k, 0, many_y, :, units(u)], hid.at[k, 0, :, :, units(u)]
+            local(some, some, h_sem.at[0, k, u]).wait()
+            local(full, full, i_sem.at[0, k, u]).wait()
     for h in range(PIECES):
         for k in range(2):
-            for c in range(2):
-                local(orecv.at[h, k, c, many_x], orecv.at[h, k, c, many_x], o_sem.at[0, h, k, c]).wait()
+            local(orecv.at[h, k, many_x], orecv.at[h, k, many_x], o_sem.at[0, h, k]).wait()
         for step in range(ups):
             local(up_sum.at[h, 0], up_sum.at[h, 0], pu_sem.at[0, h, step]).wait()
         for step in range(downs):
@@ -546,7 +563,7 @@
     ne, nf = nz * nx, 2 * ny
     gt, gs = nf * TOK, nf * CAP
     half, hidden, ups = nz * gs // 2, ne * unit, nz // 2
-    chunk, hw, span = half // 2, fs // PIECES, unit * (fs // BLOCK)
+    hw, span = fs // PIECES, unit * (fs // BLOCK)
     np = len(PARTS)
     vm = pl.BlockSpec(memory_space=pltpu.VMEM)
     hbm = pl.BlockSpec(memory_space=pltpu.HBM)
@@ -554,7 +571,7 @@
     V = lambda *s: pltpu.VMEM(s, BF)
     W = lambda *s: pltpu.VMEM(s, F32)
     dma = lambda *s: pltpu.SemaphoreType.DMA(s)
-    sums = [V(2, 2, ny, chunk, 2 * hidden)] * 4 + [V(2, 2, 2, chunk, 2 * hidden), V(2, 2, 2, chunk, hidden)]
+    sums = [V(2, ny, half, 2 * hidden)] * 4 + [V(2, 2, half, 2 * hidden), V(2, 2, half, hidden)]
     return pl.pallas_call(
         functools.partial(layer, dims),
         out_shape=(jax.ShapeDtypeStruct((2, 3, ne, unit, fs), BF), jax.ShapeDtypeStruct((TOK, nf * fs), BF)),
@@ -563,12 +580,12 @@
         scratch_shapes=[
             V(6, ne, unit, fs), pltpu.VMEM(exps.shape, jnp.int32), V(TOK, nf * fs), pltpu.VMEM(ids.shape, jnp.int32), W(*probs.shape), W(3, 2 * ne, span), W(3, 2 * ne, span), V(ne, 8, span), V(ne, 8, span),
             W(TOK, 128), W(PIECES, nz, gt, hw), V(nz, gt, fs), W(gt, 128), W(nz, 16, gt), W(nz, 16, gt),
-            V(nx, 2, nz * gs, fs), V(2, nx, nz * gs, fs), V(2 * hidden, fs), V(PIECES, hidden, hw),
+            V(nx, 2, nz * gs, fs), V(2, nx, nz * gs, fs), V(2 * hidden, fs), V(hidden, hw),
             *sums,
-            V(2, 2, 2, ny, chunk, hidden), V(PIECES, 2, 2, nx, 2 * chunk, hw), V(PIECES, 2, 2, nx, 2 * chunk, hw),
+            V(2, 2, ny, half, hidden), V(PIECES, 2, nx, 2 * half, hw), V(PIECES, 2, nx, 2 * half, hw),
             V(PIECES, 2, ups, gt, hw), V(PIECES, ups, gt, hw), V(PIECES, ups, gt, hw), V(PIECES, gt, hw),
             dma(6), dma(4), dma(np), dma(np), dma(np), dma(3), dma(3), dma(3), dma(2, 2, ups), dma(2, 2, ups), dma(3), dma(2, 2), dma(2),
-            dma(2, 2, 2), dma(2, 2, 2, 4), dma(2, 2, 2), dma(2, 2, 2), dma(2, PIECES, 2, 2), dma(PIECES, 2, 2), dma(2, PIECES, ups), dma(2, PIECES, ups), dma(3, PIECES),
+            dma(2, 2, 2), dma(2, 2, 2, 4), dma(2, 2, 2), dma(2, 2, 2), dma(2, PIECES, 2), dma(PIECES, 2), dma(2, PIECES, ups), dma(2, PIECES, ups), dma(3, PIECES),
         ],
         compiler_params=pltpu.CompilerParams(collective_id=1, has_side_effects=True, vmem_limit_bytes=VMEM_LIMIT),
         name="layer",

time: 175 us -> 177 us (1.011)
  Pallas kernels: 168 us -> 170 us
    pallas_call x1, Pallas kernels: 168 us -> 170 us  [run_layer(): pl.pallas_call(functools.partial(layer, dims), out_shape=(jax.ShapeDtypeS...]
where the time goes in v5:
time: 177 us
  Pallas kernels  170 us (96%)
  local copies, waits for them, and re-layouts  6.18 us (3%)
    pallas_call x1, Pallas kernels, run_layer(): pl.pallas_call(functools.partial(layer, dims), out_shape=(jax.ShapeDtypeS...  170 us
    unnamed x10, local copies, waits for them, and re-layouts  6.18 us

profile of v5, /device:TPU:1, one launch (start us, length us, event | category | flops | bytes accessed | tf_op | source)
XLA Modules:
  0.0 176.9 jit_solution(344682629700307174)
XLA Ops:
  0.6 0.0 copy-start
  0.6 1.1 copy-done
  1.7 0.0 copy-start.1
  1.7 0.9 copy-done.1
  2.6 0.0 copy-start.2
  2.6 0.7 copy-done.2
  3.3 0.0 copy-start.3
  3.3 0.7 copy-done.3
  4.0 170.1 %layer.1 = (bf16[2,3,32,24,512]{4,3,2,1,0:T(8,128)(2,1)S(1)}, bf16[16,4096]{1,0:T(8,128)(2,1)S(1)}) custom-call(bf16[32,2,3,24,512]{4,3,2,1,0:T(8,128)(2,1)} %bitcast.9, s32[3,24,16,64]{3,2,1,0:T(8,128)S(1)} %bitcast.6, bf16[16,4096]{1,0:T(8,128)(2,1)S(1)} %copy-done.1, s32[8,16]{1,0:T(8,128)S(1)} %bitcast.7, f32[8,16]{1,0:T(8,128)S(1)} %bitcast.8), custom_call_target="tpu_custom_call" | custom-call | tf_op jit(solution)/shard_map/layer/pallas_call | solution.py:575
  174.1 2.2 %copy.9 = bf16[2,3,768,512]{3,2,1,0:T(8,128)(2,1)} copy(bf16[2,3,768,512]{3,2,1,0:T(8,128)(2,1)S(1)} %bitcast.5) | data formatting | bytes 9437184
  176.2 0.7 copy.10
Async XLA Ops:
  0.6 1.1 copy-start
  1.7 0.9 copy-start.1
  2.6 0.7 copy-start.2
  3.3 0.7 copy-start.3

commit v6 on v4

--- a/solution.py
+++ b/solution.py
@@ -329,11 +329,7 @@
     def first_sums(k):
         elements_wait(2 * k + 1)
         widen(2 * k + 1, wgu, hidden)
-        for c in range(2):
-            gate_up(k, c, pa, 1 - core, hidden)
-            to_fsdp(pa.at[k, c], ra.at[k, c], a_sem.at[0, k, c], a_sem.at[1, k, c], mate).start()
-            gate_up(k, c, pb, core, hidden)
-        for c in range(2):
+        def collect(c):
             local(pa.at[k, c], ra.at[k, c], a_sem.at[1, k, c]).wait()
             for j in ((2, 1, 3, 0) if ny == 4 else (1, 0)):
                 to = lax.rem(y + j, ny)
@@ -344,6 +340,14 @@
                         to_fsdp(side, rl.at[k, c, d], b_sem.at[0, k, c, d], b_sem.at[1, k, c, d], beside(d)).start()
             if ny != 4:
                 to_fsdp(rb.at[k, c, 1 - y], rc.at[k, c, 0], b_sem.at[0, k, c, 2], b_sem.at[1, k, c, 2], (1 - y) * 2 + core).start()
+
+        for c in range(2):
+            gate_up(k, c, pa, 1 - core, hidden)
+            to_fsdp(pa.at[k, c], ra.at[k, c], a_sem.at[0, k, c], a_sem.at[1, k, c], mate).start()
+            gate_up(k, c, pb, core, hidden)
+            if c == 0:
+                collect(0)
+        collect(1)
 
     def beside(d):
         return lax.rem(y + (1 if d == 0 else ny - 1), ny) * 2 + core

time: 175 us -> 174 us (level)
  no operation moved by 1% of the time
where the time goes in v6:
time: 174 us
  Pallas kernels  167 us (96%)
  local copies, waits for them, and re-layouts  6.18 us (4%)
    pallas_call x1, Pallas kernels, run_layer(): pl.pallas_call(functools.partial(layer, dims), out_shape=(jax.ShapeDtypeS...  167 us
    unnamed x10, local copies, waits for them, and re-layouts  6.18 us

profile of v6, /device:TPU:1, one launch (start us, length us, event | category | flops | bytes accessed | tf_op | source)
XLA Modules:
  0.0 174.1 jit_solution(4532635385259719647)
XLA Ops:
  0.6 0.0 copy-start
  0.6 1.1 copy-done
  1.7 0.0 copy-start.1
  1.7 0.9 copy-done.1
  2.6 0.0 copy-start.2
  2.6 0.7 copy-done.2
  3.3 0.0 copy-start.3
  3.3 0.7 copy-done.3
  4.0 167.3 %layer.1 = (bf16[2,3,32,24,512]{4,3,2,1,0:T(8,128)(2,1)S(1)}, bf16[16,4096]{1,0:T(8,128)(2,1)S(1)}) custom-call(bf16[32,2,3,24,512]{4,3,2,1,0:T(8,128)(2,1)} %bitcast.9, s32[3,24,16,64]{3,2,1,0:T(8,128)S(1)} %bitcast.6, bf16[16,4096]{1,0:T(8,128)(2,1)S(1)} %copy-done.1, s32[8,16]{1,0:T(8,128)S(1)} %bitcast.7, f32[8,16]{1,0:T(8,128)S(1)} %bitcast.8), custom_call_target="tpu_custom_call" | custom-call | tf_op jit(solution)/shard_map/layer/pallas_call | solution.py:562
  171.3 2.2 %copy.9 = bf16[2,3,768,512]{3,2,1,0:T(8,128)(2,1)} copy(bf16[2,3,768,512]{3,2,1,0:T(8,128)(2,1)S(1)} %bitcast.5) | data formatting | bytes 9437184
  173.5 0.7 copy.10
Async XLA Ops:
  0.6 1.1 copy-start
  1.7 0.9 copy-start.1
  2.6 0.7 copy-start.2
  3.3 0.7 copy-start.3
